TPU v7x, 256 devices: a whole 4x4x8 slice. The times are simulated.
256 devices in a mesh: phi: 32 (over z, x), row: 2 (over core), theta: 4 (over y).
Axes of the slice: x: 4, y: 4, z: 8, core: 2. Of those that a mesh axis runs over, the one named last changes fastest.
Arguments:
- density: float32 [16, 32, 4096], P('theta', 'row', 'phi'), may hold values from 0.5 to 2
- energy: float32 [16, 32, 4096], P('theta', 'row', 'phi'), may hold values from 0.5 to 2.5
- velocity: float32 [3, 16, 32, 4096], P(None, 'theta', 'row', 'phi'), may hold values from -1.2 to 1.2
- shifts: int32 [32], P('row'), may hold values from 0 to 4095, as said below
- viscosity: float32 [32], P('row'), may hold values from 0.05 to 0.3
Outputs:
- density_out: float32 [16, 32, 4096], P('theta', 'row', 'phi')
- energy_out: float32 [16, 32, 4096], P('theta', 'row', 'phi')
- velocity_out: float32 [3, 16, 32, 4096], P(None, 'theta', 'row', 'phi')
Inputs may be any that keep to these rules, and one draw needn't show every extreme that they name: `shifts`: in each aligned block of 16 radii at least one radius has an offset between 1984 and 2111, and at least one radius has an offset between 1 and 64.
All inputs are finite; a program needn't handle non-finite values.
Results may differ from a plain program's by a relative error of at most 0.00002.
Values sent between devices are 32-bit elements; how exact they have to be, the bound alone decides.
No kernel may reach another device: no remote copies, remote signals or barrier semaphores. Data moves between devices by JAX's collectives and lax.ppermute only.
A program may use at most 64 MiB of HBM per device.

v0:
```python
import jax
import jax.numpy as jnp
from jax import lax
from jax.sharding import PartitionSpec as P

GAMMA_LESS = 0.4
TIME_STEP = 0.4
DAMPING = 1.0
ROTATION = 0.5


def padded_2(value, sides, width, wrap):
    for axis, dim in sides:
        devices, length = (lax.axis_size(axis), value.shape[dim])
        up = [(i, (i + 1) % devices) for i in range(devices if wrap else devices - 1)]
        down = [(j, i) for i, j in up]
        last = lax.slice_in_dim(value, length - width, length, axis=dim)
        first = lax.slice_in_dim(value, 0, width, axis=dim)
        before = lax.ppermute(last, axis, up)
        after = lax.ppermute(first, axis, down)
        value = jnp.concatenate([before, value, after], axis=dim)
    return value


def from_behind(value, axis, by):
    devices = lax.axis_size(axis)
    return lax.ppermute(value, axis, [(i, (i + by) % devices) for i in range(devices)])


def face_flux(quantity_lo, quantity_hi, speed_lo, speed_hi):
    return 0.25 * (speed_lo + speed_hi) * (quantity_lo + quantity_hi) - 0.5 * DAMPING * (
        quantity_hi - quantity_lo
    )


def segment_rates(padded, inv_rho):
    density, energy, radial_v, polar_v, azimuth_v = (
        padded[0],
        padded[1],
        padded[2],
        padded[3],
        padded[4],
    )

    def interior(quantity):
        return quantity[1:-1, 1:-1]

    def radial(quantity):
        fluxes = face_flux(
            quantity[1:-1, :-1], quantity[1:-1, 1:], radial_v[1:-1, :-1], radial_v[1:-1, 1:]
        )
        return fluxes[:, 1:] - fluxes[:, :-1]

    def polar(quantity):
        fluxes = face_flux(
            quantity[:-1, 1:-1], quantity[1:, 1:-1], polar_v[:-1, 1:-1], polar_v[1:, 1:-1]
        )
        return fluxes[1:] - fluxes[:-1]

    def laplace(quantity):
        return (
            quantity[2:, 1:-1]
            + quantity[:-2, 1:-1]
            + quantity[1:-1, 2:]
            + quantity[1:-1, :-2]
            - 4.0 * interior(quantity)
        )

    pressure = GAMMA_LESS * energy
    grad_radial = 0.5 * (pressure[1:-1, 2:] - pressure[1:-1, :-2])
    grad_polar = 0.5 * (pressure[2:, 1:-1] - pressure[:-2, 1:-1])
    rate_rho = -(radial(density) + polar(density))
    rate_energy = -(radial(energy) + polar(energy))
    rate_radial = (
        -grad_radial * inv_rho
        + 0.5 * DAMPING * laplace(radial_v)
        + 2.0 * ROTATION * interior(azimuth_v)
    )
    rate_polar = -grad_polar * inv_rho + 0.5 * DAMPING * laplace(polar_v)
    rate_azimuth = -(radial(azimuth_v) + polar(azimuth_v)) - 0.5 * ROTATION * interior(radial_v)
    return jnp.stack([rate_rho, rate_energy, rate_radial, rate_polar, rate_azimuth])


def per_device(density, energy, velocity, shifts, viscosity):
    fields = jnp.concatenate([density[None], energy[None], velocity], 0)
    inv_rho = 1.0 / density
    theta_len = density.shape[0]
    radial_len = density.shape[1]
    shard_len = density.shape[2]
    deep_fields = padded_2(fields, (("row", 2), ("theta", 1)), 2, False)
    polar_pos = lax.axis_index("theta") * theta_len - 1 + lax.iota(jnp.int32, theta_len + 2)
    radial_pos = lax.axis_index("row") * radial_len - 1 + lax.iota(jnp.int32, radial_len + 2)
    polar_in = (polar_pos >= 0) & (polar_pos < theta_len * lax.axis_size("theta"))
    radial_in = (radial_pos >= 0) & (radial_pos < radial_len * lax.axis_size("row"))
    inside = polar_in[:, None, None] & radial_in[None, :, None]
    rho_wide = deep_fields[0, 1:-1, 1:-1]
    inv_wide = jnp.where(inside, 1.0 / jnp.where(inside, rho_wide, 1.0), 0.0)
    segment_one = deep_fields[:, 1:-1, 1:-1] + TIME_STEP * segment_rates(deep_fields, inv_wide)
    segment_one = jnp.where(inside[None], segment_one, 0.0)
    segment_two = 0.5 * (
        fields + segment_one[:, 1:-1, 1:-1] + TIME_STEP * segment_rates(segment_one, inv_rho)
    )
    shard_hops = shifts // shard_len
    remainder = shifts - shard_hops * shard_len
    rotated = segment_two
    for bit_index in range(lax.axis_size("phi").bit_length() - 1):
        hopped = from_behind(rotated, "phi", 1 << bit_index)
        chosen = shard_hops >> bit_index & 1 == 1
        rotated = jnp.where(chosen[None, None, :, None], hopped, rotated)
    further = from_behind(rotated, "phi", 1)
    combined = jnp.concatenate([further, rotated], 3)
    shifted = jax.vmap(
        lambda annulus, offset: lax.dynamic_slice_in_dim(
            annulus, shard_len - offset, shard_len, axis=2
        ),
        in_axes=(2, 0),
        out_axes=2,
    )(combined, remainder)
    padded = padded_2(shifted, (("phi", 3),), 1, True)
    behind = padded[..., :-2]
    ahead = padded[..., 2:]
    visc_coef = viscosity[None, :, None]
    velocity_out = shifted[2:] + visc_coef * (ahead[2:] - 2.0 * shifted[2:] + behind[2:])
    azimuth_slope = 0.5 * (ahead[4] - behind[4])
    energy_out = shifted[1] + visc_coef * shifted[0] * azimuth_slope * azimuth_slope
    return (shifted[0], energy_out, velocity_out)


def solution(mesh):
    return jax.shard_map(
        per_device,
        mesh=mesh,
        in_specs=(
            P("theta", "row", "phi"),
            P("theta", "row", "phi"),
            P(None, "theta", "row", "phi"),
            P("row"),
            P("row"),
        ),
        out_specs=(
            P("theta", "row", "phi"),
            P("theta", "row", "phi"),
            P(None, "theta", "row", "phi"),
        ),
        check_vma=False,
    )
```

profile of v0, /device:TPU:24, one launch (start us, length us, event | category | flops | bytes accessed | tf_op | source)
XLA Modules:
  0.0 108.2 jit_solution(7353969330222820936)
XLA Ops:
  0.7 1.0 pad_maximum_fusion.2
  1.7 1.3 %collective-permute-start.1 = (f32[5,4,2,128]{3,2,1,0:T(2,128)S(1)}, f32[5,4,2,128]{3,2,1,0:T(2,128)S(1)}, u32[]{:S(2)}, u32[]{:S(2)}) collective-permute-start(f32[5,4,2,128]{3,2,1,0:T(2,128)S(1)} %get-tuple-element.77), channel_id=1, source_target_pairs={{4,0},{5,1},{6,2},{7,3},{12,8},{13,9},{14,10},{15,11},{20,16},{21,... | collective-permute-start | bytes 61448 | tf_op jit(solution)/shard_map/ppermute | solution.py:20
  3.0 3.0 %collective-permute-start = (f32[5,4,2,128]{3,2,1,0:T(2,128)S(1)}, f32[5,4,2,128]{3,2,1,0:T(2,128)S(1)}, u32[]{:S(2)}, u32[]{:S(2)}) collective-permute-start(f32[5,4,2,128]{3,2,1,0:T(2,128)S(1)} %get-tuple-element.78), channel_id=1, source_target_pairs={{0,4},{1,5},{2,6},{3,7},{8,12},{9,13},{10,14},{11,15},{16,20},{17,... | collective-permute-start | bytes 61448 | tf_op jit(solution)/shard_map/ppermute | solution.py:19
  6.0 0.1 broadcast_and_fusion
  6.1 0.7 collective-permute-done
  6.8 0.1 copy_dynamic-update-slice_fusion
  6.9 0.0 collective-permute-done.1
  6.9 0.1 fusion.67
  7.0 1.3 %collective-permute-start.2 = (f32[5,2,20,128]{3,1,2,0:T(2,128)S(1)}, f32[5,2,20,128]{3,1,2,0:T(2,128)S(1)}, u32[]{:S(2)}, u32[]{:S(2)}) collective-permute-start(f32[5,2,20,128]{3,1,2,0:T(2,128)S(1)} %get-tuple-element.73), channel_id=1, source_target_pairs={{0,1},{1,2},{2,3},{4,5},{5,6},{6,7},{8,9},{9,10},{10,11},{12,13},{... | collective-permute-start | bytes 307208 | tf_op jit(solution)/shard_map/ppermute | solution.py:19
  8.3 4.6 %collective-permute-start.3 = (f32[5,2,20,128]{3,1,2,0:T(2,128)S(1)}, f32[5,2,20,128]{3,1,2,0:T(2,128)S(1)}, u32[]{:S(2)}, u32[]{:S(2)}) collective-permute-start(f32[5,2,20,128]{3,1,2,0:T(2,128)S(1)} %get-tuple-element.74), channel_id=1, source_target_pairs={{1,0},{2,1},{3,2},{5,4},{6,5},{7,6},{9,8},{10,9},{11,10},{13,12},{... | collective-permute-start | bytes 307208 | tf_op jit(solution)/shard_map/ppermute | solution.py:20
  12.9 0.7 fusion.66
  13.6 0.1 copy.632
  13.7 0.4 collective-permute-done.2
  14.0 1.2 %collective-permute-done.3 = f32[5,2,20,128]{3,1,2,0:T(2,128)S(1)} collective-permute-done((f32[5,2,20,128]{3,1,2,0:T(2,128)S(1)}, f32[5,2,20,128]{3,1,2,0:T(2,128)S(1)}, u32[]{:S(2)}, u32[]{:S(2)}) %collective-permute-start.3) | collective-permute-done | bytes 102432 | tf_op jit(solution)/shard_map/ppermute | solution.py:20
  15.2 0.1 pad_maximum_fusion
  15.5 0.1 multiply_subtract_fusion.3
  15.5 0.1 multiply_subtract_fusion
  15.7 0.1 fusion.13
  15.9 0.1 fusion
  16.4 0.1 fusion.2
  16.4 1.6 %collective-permute-start.4 = (f32[5,4,16,128]{3,2,1,0:T(8,128)S(1)}, f32[5,4,16,128]{3,2,1,0:T(8,128)S(1)}, u32[]{:S(2)}, u32[]{:S(2)}) collective-permute-start(f32[5,4,16,128]{3,2,1,0:T(8,128)S(1)} %fusion.2), channel_id=1, source_target_pairs={{0,8},{8,16},{16,24},{24,32},{32,40},{40,48},{48,56},{56,64},{64,7... | collective-permute-start | bytes 491528 | tf_op jit(solution)/shard_map/ppermute | solution.py:27
  18.0 10.0 %collective-permute-done.4 = f32[5,4,16,128]{3,2,1,0:T(8,128)S(1)} collective-permute-done((f32[5,4,16,128]{3,2,1,0:T(8,128)S(1)}, f32[5,4,16,128]{3,2,1,0:T(8,128)S(1)}, u32[]{:S(2)}, u32[]{:S(2)}) %collective-permute-start.4) | collective-permute-done | bytes 163872 | tf_op jit(solution)/shard_map/ppermute | solution.py:27
  28.0 0.1 broadcast_select_fusion
  28.1 0.0 copy-start.3
  28.1 0.1 collective-permute-start.5
  28.2 10.1 %collective-permute-done.5 = f32[5,4,16,128]{3,2,1,0:T(8,128)S(1)} collective-permute-done((f32[5,4,16,128]{3,2,1,0:T(8,128)S(1)}, f32[5,4,16,128]{3,2,1,0:T(8,128)S(1)}, u32[]{:S(2)}, u32[]{:S(2)}) %collective-permute-start.5) | collective-permute-done | bytes 163872 | tf_op jit(solution)/shard_map/ppermute | solution.py:27
  38.3 0.1 broadcast_select_fusion.1
  38.4 0.1 collective-permute-start.6
  38.5 9.2 %collective-permute-done.6 = f32[5,4,16,128]{3,2,1,0:T(8,128)S(1)} collective-permute-done((f32[5,4,16,128]{3,2,1,0:T(8,128)S(1)}, f32[5,4,16,128]{3,2,1,0:T(8,128)S(1)}, u32[]{:S(2)}, u32[]{:S(2)}) %collective-permute-start.6) | collective-permute-done | bytes 163872 | tf_op jit(solution)/shard_map/ppermute | solution.py:27
  47.7 0.1 broadcast_select_fusion.2
  47.8 0.1 collective-permute-start.7
  47.9 11.4 %collective-permute-done.7 = f32[5,4,16,128]{3,2,1,0:T(8,128)S(1)} collective-permute-done((f32[5,4,16,128]{3,2,1,0:T(8,128)S(1)}, f32[5,4,16,128]{3,2,1,0:T(8,128)S(1)}, u32[]{:S(2)}, u32[]{:S(2)}) %collective-permute-start.7) | collective-permute-done | bytes 163872 | tf_op jit(solution)/shard_map/ppermute | solution.py:27
  59.3 0.1 broadcast_select_fusion.3
  59.4 3.6 %collective-permute-start.8 = (f32[5,4,16,128]{3,2,1,0:T(8,128)S(1)}, f32[5,4,16,128]{3,2,1,0:T(8,128)S(1)}, u32[]{:S(2)}, u32[]{:S(2)}) collective-permute-start(f32[5,4,16,128]{3,2,1,0:T(8,128)S(1)} %broadcast_select_fusion.3), channel_id=1, source_target_pairs={{0,128},{8,136},{16,144},{24,152},{32,160},{40,168},{48,176},{56,1... | collective-permute-start | bytes 491528 | tf_op jit(solution)/shard_map/ppermute | solution.py:27
  62.9 6.5 %collective-permute-done.8 = f32[5,4,16,128]{3,2,1,0:T(8,128)S(1)} collective-permute-done((f32[5,4,16,128]{3,2,1,0:T(8,128)S(1)}, f32[5,4,16,128]{3,2,1,0:T(8,128)S(1)}, u32[]{:S(2)}, u32[]{:S(2)}) %collective-permute-start.8) | collective-permute-done | bytes 163872 | tf_op jit(solution)/shard_map/ppermute | solution.py:27
  69.4 0.1 broadcast_select_fusion.4
  69.5 0.1 collective-permute-start.9
  69.6 8.6 %collective-permute-done.9 = f32[5,4,16,128]{3,2,1,0:T(8,128)S(1)} collective-permute-done((f32[5,4,16,128]{3,2,1,0:T(8,128)S(1)}, f32[5,4,16,128]{3,2,1,0:T(8,128)S(1)}, u32[]{:S(2)}, u32[]{:S(2)}) %collective-permute-start.9) | collective-permute-done | bytes 163872 | tf_op jit(solution)/shard_map/ppermute | solution.py:27
  78.3 7.6 %copy.638 = f32[5,4,16,256]{0,1,2,3:T(4,128)} copy(f32[5,4,16,256]{3,2,1,0:T(8,128)S(1)} %pad_maximum_fusion.1) | data formatting | bytes 655360 | tf_op jit(solution)/shard_map/concatenate | solution.py:111
  85.9 9.0 %gather_fusion = f32[16,5,4,128]{1,2,3,0:T(4,128)} fusion(f32[16,5,4,256]{1,2,0,3:T(4,128)} %bitcast.88, s32[16]{0:T(128)S(1)} %get-tuple-element.59), kind=kCustom, calls=%fused_computation | custom fusion | bytes 327936 | tf_op jit(solution)/shard_map/vmap()/gather | solution.py:113
  94.9 2.9 %copy.639 = f32[16,5,4,128]{3,0,2,1:T(8,128)S(1)} copy(f32[16,5,4,128]{1,2,3,0:T(4,128)} %gather_fusion) | data formatting | bytes 327680 | tf_op jit(solution)/shard_map/vmap()/gather | solution.py:113
  97.7 0.1 fusion.68
  97.9 0.1 collective-permute-start.10
  97.9 2.0 %collective-permute-start.11 = (f32[5,4,16,1]{3,2,1,0:T(8,128)S(1)}, f32[5,4,16,1]{3,2,1,0:T(8,128)S(1)}, u32[]{:S(2)}, u32[]{:S(2)}) collective-permute-start(f32[5,4,16,1]{3,2,1,0:T(8,128)S(1)} %get-tuple-element.76), channel_id=1, source_target_pairs={{0,8},{8,16},{16,24},{24,32},{32,40},{40,48},{48,56},{56,64},{64,7... | collective-permute-start | bytes 3848 | tf_op jit(solution)/shard_map/ppermute | solution.py:19
  100.0 3.3 %collective-permute-done.10 = f32[5,4,16,1]{3,2,1,0:T(8,128)S(1)} collective-permute-done((f32[5,4,16,1]{3,2,1,0:T(8,128)S(1)}, f32[5,4,16,1]{3,2,1,0:T(8,128)S(1)}, u32[]{:S(2)}, u32[]{:S(2)}) %collective-permute-start.10) | collective-permute-done | bytes 1312 | tf_op jit(solution)/shard_map/ppermute | solution.py:20
  103.2 3.4 %collective-permute-done.11 = f32[5,4,16,1]{3,2,1,0:T(8,128)S(1)} collective-permute-done((f32[5,4,16,1]{3,2,1,0:T(8,128)S(1)}, f32[5,4,16,1]{3,2,1,0:T(8,128)S(1)}, u32[]{:S(2)}, u32[]{:S(2)}) %collective-permute-start.11) | collective-permute-done | bytes 1312 | tf_op jit(solution)/shard_map/ppermute | solution.py:19
  106.7 0.7 fusion.33
  107.4 0.8 fusion.5
  (33 shorter events, 0.6 us)
Async XLA Ops:
  0.6 15.6 %copy-start = (f32[4,16,128]{2,1,0:T(8,128)S(1)}, f32[4,16,128]{2,1,0:T(8,128)}, u32[]{:S(2)}) copy-start(f32[4,16,128]{2,1,0:T(8,128)} %param.5) | copy-start | bytes 98308
  0.6 15.7 %copy-start.1 = (f32[3,4,16,128]{3,2,1,0:T(8,128)S(1)}, f32[3,4,16,128]{3,2,1,0:T(8,128)}, u32[]{:S(2)}) copy-start(f32[3,4,16,128]{3,2,1,0:T(8,128)} %param.7) | copy-start | bytes 294916
  0.7 15.7 %copy-start.2 = (f32[4,16,128]{2,1,0:T(8,128)S(1)}, f32[4,16,128]{2,1,0:T(8,128)}, u32[]{:S(2)}) copy-start(f32[4,16,128]{2,1,0:T(8,128)} %param.6) | copy-start | bytes 98308
  1.7 5.2 %collective-permute-start.1 = (f32[5,4,2,128]{3,2,1,0:T(2,128)S(1)}, f32[5,4,2,128]{3,2,1,0:T(2,128)S(1)}, u32[]{:S(2)}, u32[]{:S(2)}) collective-permute-start(f32[5,4,2,128]{3,2,1,0:T(2,128)S(1)} %get-tuple-element.77), channel_id=1, source_target_pairs={{4,0},{5,1},{6,2},{7,3},{12,8},{13,9},{14,10},{15,11},{20,16},{21,... | collective-permute-start | bytes 61448 | tf_op jit(solution)/shard_map/ppermute | solution.py:20
  3.0 3.9 %collective-permute-start = (f32[5,4,2,128]{3,2,1,0:T(2,128)S(1)}, f32[5,4,2,128]{3,2,1,0:T(2,128)S(1)}, u32[]{:S(2)}, u32[]{:S(2)}) collective-permute-start(f32[5,4,2,128]{3,2,1,0:T(2,128)S(1)} %get-tuple-element.78), channel_id=1, source_target_pairs={{0,4},{1,5},{2,6},{3,7},{8,12},{9,13},{10,14},{11,15},{16,20},{17,... | collective-permute-start | bytes 61448 | tf_op jit(solution)/shard_map/ppermute | solution.py:19
  7.0 7.0 %collective-permute-start.2 = (f32[5,2,20,128]{3,1,2,0:T(2,128)S(1)}, f32[5,2,20,128]{3,1,2,0:T(2,128)S(1)}, u32[]{:S(2)}, u32[]{:S(2)}) collective-permute-start(f32[5,2,20,128]{3,1,2,0:T(2,128)S(1)} %get-tuple-element.73), channel_id=1, source_target_pairs={{0,1},{1,2},{2,3},{4,5},{5,6},{6,7},{8,9},{9,10},{10,11},{12,13},{... | collective-permute-start | bytes 307208 | tf_op jit(solution)/shard_map/ppermute | solution.py:19
  8.3 6.9 %collective-permute-start.3 = (f32[5,2,20,128]{3,1,2,0:T(2,128)S(1)}, f32[5,2,20,128]{3,1,2,0:T(2,128)S(1)}, u32[]{:S(2)}, u32[]{:S(2)}) collective-permute-start(f32[5,2,20,128]{3,1,2,0:T(2,128)S(1)} %get-tuple-element.74), channel_id=1, source_target_pairs={{1,0},{2,1},{3,2},{5,4},{6,5},{7,6},{9,8},{10,9},{11,10},{13,12},{... | collective-permute-start | bytes 307208 | tf_op jit(solution)/shard_map/ppermute | solution.py:20
  16.4 11.6 %collective-permute-start.4 = (f32[5,4,16,128]{3,2,1,0:T(8,128)S(1)}, f32[5,4,16,128]{3,2,1,0:T(8,128)S(1)}, u32[]{:S(2)}, u32[]{:S(2)}) collective-permute-start(f32[5,4,16,128]{3,2,1,0:T(8,128)S(1)} %fusion.2), channel_id=1, source_target_pairs={{0,8},{8,16},{16,24},{24,32},{32,40},{40,48},{48,56},{56,64},{64,7... | collective-permute-start | bytes 491528 | tf_op jit(solution)/shard_map/ppermute | solution.py:27
  28.1 78.6 %copy-start.3 = (f32[16]{0:T(128)S(1)}, f32[16]{0:T(128)}, u32[]{:S(2)}) copy-start(f32[16]{0:T(128)} %param.9) | copy-start | bytes 196
  28.1 10.2 %collective-permute-start.5 = (f32[5,4,16,128]{3,2,1,0:T(8,128)S(1)}, f32[5,4,16,128]{3,2,1,0:T(8,128)S(1)}, u32[]{:S(2)}, u32[]{:S(2)}) collective-permute-start(f32[5,4,16,128]{3,2,1,0:T(8,128)S(1)} %broadcast_select_fusion), channel_id=1, source_target_pairs={{0,16},{8,24},{16,32},{24,40},{32,48},{40,56},{48,64},{56,72},{64,... | collective-permute-start | bytes 491528 | tf_op jit(solution)/shard_map/ppermute | solution.py:27
  38.4 9.3 %collective-permute-start.6 = (f32[5,4,16,128]{3,2,1,0:T(8,128)S(1)}, f32[5,4,16,128]{3,2,1,0:T(8,128)S(1)}, u32[]{:S(2)}, u32[]{:S(2)}) collective-permute-start(f32[5,4,16,128]{3,2,1,0:T(8,128)S(1)} %broadcast_select_fusion.1), channel_id=1, source_target_pairs={{0,32},{8,40},{16,48},{24,56},{32,64},{40,72},{48,80},{56,88},{64,... | collective-permute-start | bytes 491528 | tf_op jit(solution)/shard_map/ppermute | solution.py:27
  47.8 11.5 %collective-permute-start.7 = (f32[5,4,16,128]{3,2,1,0:T(8,128)S(1)}, f32[5,4,16,128]{3,2,1,0:T(8,128)S(1)}, u32[]{:S(2)}, u32[]{:S(2)}) collective-permute-start(f32[5,4,16,128]{3,2,1,0:T(8,128)S(1)} %broadcast_select_fusion.2), channel_id=1, source_target_pairs={{0,64},{8,72},{16,80},{24,88},{32,96},{40,104},{48,112},{56,120},{... | collective-permute-start | bytes 491528 | tf_op jit(solution)/shard_map/ppermute | solution.py:27
  59.4 10.1 %collective-permute-start.8 = (f32[5,4,16,128]{3,2,1,0:T(8,128)S(1)}, f32[5,4,16,128]{3,2,1,0:T(8,128)S(1)}, u32[]{:S(2)}, u32[]{:S(2)}) collective-permute-start(f32[5,4,16,128]{3,2,1,0:T(8,128)S(1)} %broadcast_select_fusion.3), channel_id=1, source_target_pairs={{0,128},{8,136},{16,144},{24,152},{32,160},{40,168},{48,176},{56,1... | collective-permute-start | bytes 491528 | tf_op jit(solution)/shard_map/ppermute | solution.py:27
  69.5 8.7 %collective-permute-start.9 = (f32[5,4,16,128]{3,2,1,0:T(8,128)S(1)}, f32[5,4,16,128]{3,2,1,0:T(8,128)S(1)}, u32[]{:S(2)}, u32[]{:S(2)}) collective-permute-start(f32[5,4,16,128]{3,2,1,0:T(8,128)S(1)} %broadcast_select_fusion.4), channel_id=1, source_target_pairs={{0,8},{8,16},{16,24},{24,32},{32,40},{40,48},{48,56},{56,64},{64,7... | collective-permute-start | bytes 491528 | tf_op jit(solution)/shard_map/ppermute | solution.py:27
  97.9 5.4 %collective-permute-start.10 = (f32[5,4,16,1]{3,2,1,0:T(8,128)S(1)}, f32[5,4,16,1]{3,2,1,0:T(8,128)S(1)}, u32[]{:S(2)}, u32[]{:S(2)}) collective-permute-start(f32[5,4,16,1]{3,2,1,0:T(8,128)S(1)} %get-tuple-element.75), channel_id=1, source_target_pairs={{8,0},{16,8},{24,16},{32,24},{40,32},{48,40},{56,48},{64,56},{72,6... | collective-permute-start | bytes 3848 | tf_op jit(solution)/shard_map/ppermute | solution.py:20
  97.9 8.7 %collective-permute-start.11 = (f32[5,4,16,1]{3,2,1,0:T(8,128)S(1)}, f32[5,4,16,1]{3,2,1,0:T(8,128)S(1)}, u32[]{:S(2)}, u32[]{:S(2)}) collective-permute-start(f32[5,4,16,1]{3,2,1,0:T(8,128)S(1)} %get-tuple-element.76), channel_id=1, source_target_pairs={{0,8},{8,16},{16,24},{24,32},{32,40},{40,48},{48,56},{56,64},{64,7... | collective-permute-start | bytes 3848 | tf_op jit(solution)/shard_map/ppermute | solution.py:19
where the time goes:
time: 110 us; the launch traced here: 108 us
  waiting for transfers between devices  64.8 us (59%)
  local copies, waits for them, and re-layouts  20.1 us (18%)
  starting transfers between devices  17.7 us (16%)
  other arithmetic  4.54 us (4%)
    ppermute x6, waiting for transfers between devices, from_behind(): lax.ppermute(value, axis, [(i, (i + by) % devices) for i in range(devices)])  55.9 us
    gather x2, local copies, waits for them, and re-layouts, per_device(): lax.dynamic_slice_in_dim(annulus, shard_len - offset, shard_len, axis=2)  11.8 us
    concatenate x1, local copies, waits for them, and re-layouts, per_device(): combined = jnp.concatenate([further, rotated], 3)  7.64 us
    ppermute x3, starting transfers between devices, padded_2(): before = lax.ppermute(last, axis, up)  6.33 us
    ppermute x3, starting transfers between devices, padded_2(): after = lax.ppermute(first, axis, down)  5.93 us
    ppermute x6, starting transfers between devices, from_behind(): lax.ppermute(value, axis, [(i, (i + by) % devices) for i in range(devices)])  5.46 us
    ppermute x3, waiting for transfers between devices, padded_2(): before = lax.ppermute(last, axis, up)  4.51 us
    ppermute x3, waiting for transfers between devices, padded_2(): after = lax.ppermute(first, axis, down)  4.48 us
  transfers between devices with their start and end apart: 12, of which 11 were waited for; matrix products, arithmetic and copies ran while one was open for 1% of the time, Pallas kernels for 0%

commit v1 on v0

v1 whole, which is shorter than its diff:
```python
import jax
import jax.numpy as jnp
from jax import lax
from jax.experimental import pallas as pl
from jax.experimental.pallas import tpu as pltpu
from jax.sharding import PartitionSpec as P

GAMMA_LESS = 0.4
TIME_STEP = 0.4
DAMPING = 1.0
ROTATION = 0.5

FIELDS = 5
TH = 4
CR = 16
LANES = 128
TILE = 8
PHI = 32
PAIRS = TH * CR // PHI
ROWS = FIELDS * PAIRS


def face(q_lo, q_hi, u_lo, u_hi):
    return 0.25 * (u_lo + u_hi) * (q_lo + q_hi) - 0.5 * DAMPING * (q_hi - q_lo)


def up(value):
    return pltpu.roll(value, value.shape[0] - 1, 0)


def down(value):
    return pltpu.roll(value, 1, 0)


def rates(field, inv_rho, t):
    rho, en, vr, vt, vp = (field[f] for f in range(FIELDS))
    vr_hi = up(vr[t])
    out = []

    def divergence(q, q_hi):
        flux = face(q[t], q_hi, vr[t], vr_hi)
        radial = flux - down(flux)
        polar = face(q[t], q[t + 1], vt[t], vt[t + 1]) - face(q[t - 1], q[t], vt[t - 1], vt[t])
        return radial + polar

    en_hi = up(en[t])
    d_rho = -divergence(rho, up(rho[t]))
    d_en = -divergence(en, en_hi)
    d_vp = -divergence(vp, up(vp[t])) - 0.5 * ROTATION * vr[t]
    grad_r = 0.5 * GAMMA_LESS * (en_hi - down(en[t]))
    grad_t = 0.5 * GAMMA_LESS * (en[t + 1] - en[t - 1])
    lap_r = vr[t + 1] + vr[t - 1] + vr_hi + down(vr[t]) - 4.0 * vr[t]
    lap_t = vt[t + 1] + vt[t - 1] + up(vt[t]) + down(vt[t]) - 4.0 * vt[t]
    d_vr = -grad_r * inv_rho + 0.5 * DAMPING * lap_r + 2.0 * ROTATION * vp[t]
    d_vt = -grad_t * inv_rho + 0.5 * DAMPING * lap_t
    return d_rho, d_en, d_vr, d_vt, d_vp


def stencil_kernel(rho_ref, en_ref, vel_ref, lo_ref, hi_ref, side_ref, out_ref):
    row = lax.axis_index("row")
    theta = lax.axis_index("theta")
    pos = lax.broadcasted_iota(jnp.int32, (TILE, LANES), 0)
    near = jnp.where(row == 0, pos, TILE - 1 - pos) < TILE // 2

    def own(f, t):
        if t < 2:
            return lo_ref[f, t]
        if t >= TH + 2:
            return hi_ref[f, t - TH - 2]
        t -= 2
        return rho_ref[t] if f == 0 else en_ref[t] if f == 1 else vel_ref[f - 2, t]

    def wide(f, t):
        return jnp.concatenate([own(f, t), jnp.where(near, side_ref[f, t], 0.0)], 0)

    field = [[wide(f, t) for t in range(TH + 4)] for f in range(FIELDS)]
    first = [[None] * (TH + 4) for _ in range(FIELDS)]
    side_in = jnp.concatenate([jnp.ones((CR, LANES), jnp.bool_), near], 0)
    inverse = [None] * (TH + 4)
    for t in range(1, TH + 3):
        inside = side_in
        if t == 1:
            inside = side_in & (theta > 0)
        if t == TH + 2:
            inside = side_in & (theta < lax.axis_size("theta") - 1)
        inverse[t] = 1.0 / jnp.where(inside, field[0][t], 1.0)
        steps = rates(field, inverse[t], t)
        for f in range(FIELDS):
            first[f][t] = jnp.where(inside, field[f][t] + TIME_STEP * steps[f], 0.0)
    for t in range(2, TH + 2):
        steps = rates(first, inverse[t], t)
        for f in range(FIELDS):
            second = 0.5 * (field[f][t] + first[f][t] + TIME_STEP * steps[f])
            for p in range(PAIRS):
                start = (t - 2) * TILE * ROWS + f * PAIRS + p
                out_ref[pl.ds(start, TILE, stride=ROWS), :] = second[p * TILE : (p + 1) * TILE]


def rotate_kernel(shift_ref, visc_ref, in_ref, out_ref, twice_ref):
    mine = lax.axis_index("phi") % TILE
    lane = lax.broadcasted_iota(jnp.int32, (PHI, LANES), 1)
    for p in range(PAIRS):
        radius = mine + p * TILE
        shift = shift_ref[radius]
        nu = visc_ref[radius]
        hops = lax.shift_right_logical(shift, 7)
        rest = jnp.bitwise_and(shift, LANES - 1)
        wrapped = lane < rest

        def shifted(f):
            turned = pltpu.roll(in_ref[pl.ds(f * PAIRS + p, PHI, stride=ROWS), :], rest, 1)
            slot = f * PAIRS + p
            twice_ref[slot, :PHI] = turned
            twice_ref[slot, PHI:] = turned
            near = twice_ref[slot, pl.ds(PHI - hops, PHI), :]
            far = twice_ref[slot, pl.ds(PHI - 1 - hops, PHI), :]
            return jnp.where(wrapped, far, near)

        def put(f, value):
            out_ref[pl.ds(f * PAIRS + p, PHI, stride=ROWS), :] = value

        def sides(value):
            right = pltpu.roll(value, 1, 1)
            left = pltpu.roll(value, LANES - 1, 1)
            behind = jnp.where(lane == 0, pltpu.roll(right, 1, 0), right)
            ahead = jnp.where(lane == LANES - 1, pltpu.roll(left, PHI - 1, 0), left)
            return behind, ahead

        rho = shifted(0)
        put(0, rho)
        for f in range(2, FIELDS):
            value = shifted(f)
            behind, ahead = sides(value)
            put(f, value + nu * (ahead - 2.0 * value + behind))
            if f == FIELDS - 1:
                slope = 0.5 * (ahead - behind)
                put(1, shifted(1) + nu * rho * slope * slope)


def unpack_kernel(in_ref, rho_ref, en_ref, vel_ref):
    for f in range(FIELDS):
        for t in range(TH):
            for p in range(PAIRS):
                start = t * TILE * ROWS + f * PAIRS + p
                value = in_ref[pl.ds(start, TILE, stride=ROWS), :]
                span = slice(p * TILE, (p + 1) * TILE)
                if f == 0:
                    rho_ref[t, span] = value
                elif f == 1:
                    en_ref[t, span] = value
                else:
                    vel_ref[f - 2, t, span] = value


def vmem():
    return pl.BlockSpec(memory_space=pltpu.VMEM)


def smem():
    return pl.BlockSpec(memory_space=pltpu.SMEM)


def per_device(density, energy, velocity, shifts, viscosity):
    thetas = lax.axis_size("theta")
    rows = lax.axis_index("row")
    fields = jnp.concatenate([density[None], energy[None], velocity], 0)
    upward = [(i, i + 1) for i in range(thetas - 1)]
    downward = [(j, i) for i, j in upward]
    lo = lax.ppermute(fields[:, TH - 2 :], "theta", upward)
    hi = lax.ppermute(fields[:, :2], "theta", downward)
    tall = jnp.concatenate([lo, fields, hi], 1)
    edge = jnp.where(rows == 0, tall[:, :, CR - TILE :], tall[:, :, :TILE])
    side = lax.ppermute(edge, "row", [(0, 1), (1, 0)])
    flat = jax.ShapeDtypeStruct((PHI * ROWS, LANES), jnp.float32)
    second = pl.pallas_call(
        stencil_kernel,
        out_shape=flat,
        in_specs=[vmem()] * 6,
        out_specs=vmem(),
        name="stencil",
    )(density, energy, velocity, lo, hi, side)

    def exchange(value):
        value = lax.all_to_all(value.reshape(-1), "phi", 0, 0, tiled=True)
        return value.reshape(PHI * ROWS, LANES)

    turned = pl.pallas_call(
        rotate_kernel,
        out_shape=flat,
        in_specs=[smem(), smem(), vmem()],
        out_specs=vmem(),
        scratch_shapes=[pltpu.VMEM((ROWS, 2 * PHI, LANES), jnp.float32)],
        name="rotate",
    )(shifts, viscosity, exchange(second))
    block = jax.ShapeDtypeStruct(density.shape, jnp.float32)
    return pl.pallas_call(
        unpack_kernel,
        out_shape=(block, block, jax.ShapeDtypeStruct(velocity.shape, jnp.float32)),
        in_specs=[vmem()],
        out_specs=(vmem(), vmem(), vmem()),
        name="unpack",
    )(exchange(turned))


def solution(mesh):
    return jax.shard_map(
        per_device,
        mesh=mesh,
        in_specs=(
            P("theta", "row", "phi"),
            P("theta", "row", "phi"),
            P(None, "theta", "row", "phi"),
            P("row"),
            P("row"),
        ),
        out_specs=(
            P("theta", "row", "phi"),
            P("theta", "row", "phi"),
            P(None, "theta", "row", "phi"),
        ),
        check_vma=False,
    )
```

time: 110 us -> 57.8 us (0.53); the launches traced: 108 us -> 57.4 us
  waiting for transfers between devices: 64.8 us -> 6.41 us
  blocking collectives: 0 us -> 38.3 us
  local copies, waits for them, and re-layouts: 20.1 us -> 1.28 us
  starting transfers between devices: 17.7 us -> 4.17 us
  Pallas kernels: 0 us -> 5.59 us
  other arithmetic: 4.54 us -> 0.97 us
    ppermute x12 -> x3, waiting for transfers between devices: 64.8 us -> 6.41 us  [the longest x1 4.29 us: per_device(): lo = lax.ppermute(fields[:, TH - 2:], 'theta', upward)]
    all_to_all x0 -> x2, blocking collectives: none -> 38.3 us  [exchange(): value = lax.all_to_all(value.reshape(-1), 'phi', 0, 0, tiled=True)]
    ppermute x12 -> x3, starting transfers between devices: 17.7 us -> 4.17 us  [the longest x1 2.78 us: per_device(): hi = lax.ppermute(fields[:, :2], 'theta', downward)]
    gather x2 -> x0, local copies, waits for them, and re-layouts: 11.8 us -> none  [per_device(): lax.dynamic_slice_in_dim(annulus, shard_len - offset, shard_len, axis=2)]
    concatenate x2 -> x0, local copies, waits for them, and re-layouts: 7.65 us -> none  [the longest x1 7.64 us: per_device(): combined = jnp.concatenate([further, rotated], 3)]
    pallas_call x0 -> x3, Pallas kernels: none -> 5.59 us  [the longest x1 2.17 us: per_device(): pl.pallas_call(stencil_kernel, out_shape=flat, in_specs=[vmem()] * 6, out...]
    add x3 -> x0, other arithmetic: 1.63 us -> none  [the longest x1 0.79 us: per_device(): shifted[2:] + visc_coef * (ahead[2:] - 2.0 * shifted[2:] + behind[2:])]
    unnamed x14 -> x12, local copies, waits for them, and re-layouts: 0.15 us -> 1.26 us
  transfers between devices with their start and end apart: 12 -> 3, of which waited for: 11 -> 3; matrix products, arithmetic and copies ran while one was open for 1% -> 0% of each run, Pallas kernels for 0% -> 0%
where the time goes in v1:
time: 57.8 us; the launch traced here: 57.4 us
  blocking collectives  38.3 us (66%)
  waiting for transfers between devices  6.41 us (11%)
  Pallas kernels  5.59 us (10%)
  starting transfers between devices  4.17 us (7%)
  local copies, waits for them, and re-layouts  1.28 us (2%)
  other arithmetic  0.97 us (2%)
  between operations  0.73 us (1%)
    all_to_all x2, blocking collectives, exchange(): value = lax.all_to_all(value.reshape(-1), 'phi', 0, 0, tiled=True)  38.3 us
    ppermute x1, waiting for transfers between devices, per_device(): lo = lax.ppermute(fields[:, TH - 2:], 'theta', upward)  4.29 us
    ppermute x1, starting transfers between devices, per_device(): hi = lax.ppermute(fields[:, :2], 'theta', downward)  2.78 us
    pallas_call x1, Pallas kernels, per_device(): pl.pallas_call(stencil_kernel, out_shape=flat, in_specs=[vmem()] * 6, out...  2.17 us
    pallas_call x1, Pallas kernels, per_device(): pl.pallas_call(rotate_kernel, out_shape=flat, in_specs=[smem(), smem(), v...  1.83 us
    pallas_call x1, Pallas kernels, per_device(): pl.pallas_call(unpack_kernel, out_shape=(block, block, jax.ShapeDtypeStru...  1.59 us
    ppermute x1, waiting for transfers between devices, per_device(): side = lax.ppermute(edge, 'row', [(0, 1), (1, 0)])  1.38 us
    ppermute x1, starting transfers between devices, per_device(): lo = lax.ppermute(fields[:, TH - 2:], 'theta', upward)  1.29 us
  transfers between devices with their start and end apart: 3, of which 3 were waited for; matrix products, arithmetic and copies ran while one was open for 0% of the time, Pallas kernels for 0%

profile of v1, /device:TPU:24, one launch (start us, length us, event | category | flops | bytes accessed | tf_op | source)
XLA Modules:
  0.0 57.4 jit_solution(5711465439875544786)
XLA Ops:
  0.6 0.9 %pad_maximum_fusion.1 = f32[5,4,16,128]{3,2,1,0:T(8,128)S(1)} fusion(f32[3,4,16,128]{3,2,1,0:T(8,128)} %vel_ref.1, f32[1,4,16,128]{3,2,1,0:T(8,128)} %bitcast.12, f32[1,4,16,128]{3,2,1,0:T(8,128)} %bitcast.10), kind=kLoop, calls=%fused_computation.2 | loop fusion | flops 81920 | bytes 327680 | tf_op jit(solution)/shard_map/concatenate | solution.py:166
  1.6 0.0 copy-start
  1.6 0.0 copy-start.3
  1.6 0.0 copy-start.4
  1.6 2.8 %collective-permute-start.1 = (f32[5,2,16,128]{3,2,1,0:T(8,128)S(1)}, f32[5,2,16,128]{3,2,1,0:T(8,128)S(1)}, u32[]{:S(2)}, u32[]{:S(2)}) collective-permute-start(f32[5,2,16,128]{3,2,1,0:T(8,128)S(1)} %get-tuple-element.3), channel_id=1, source_target_pairs={{1,0},{2,1},{3,2},{5,4},{6,5},{7,6},{9,8},{10,9},{11,10},{13,12},{... | collective-permute-start | bytes 245768 | tf_op jit(solution)/shard_map/ppermute | solution.py:170
  4.4 1.3 %collective-permute-start = (f32[5,2,16,128]{3,2,1,0:T(8,128)S(1)}, f32[5,2,16,128]{3,2,1,0:T(8,128)S(1)}, u32[]{:S(2)}, u32[]{:S(2)}) collective-permute-start(f32[5,2,16,128]{3,2,1,0:T(8,128)S(1)} %get-tuple-element.4), channel_id=1, source_target_pairs={{0,1},{1,2},{2,3},{4,5},{5,6},{6,7},{8,9},{9,10},{10,11},{12,13},{... | collective-permute-start | bytes 245768 | tf_op jit(solution)/shard_map/ppermute | solution.py:169
  5.7 0.7 %collective-permute-done.1.hi_ref = f32[5,2,16,128]{3,2,1,0:T(8,128)S(1)} collective-permute-done((f32[5,2,16,128]{3,2,1,0:T(8,128)S(1)}, f32[5,2,16,128]{3,2,1,0:T(8,128)S(1)}, u32[]{:S(2)}, u32[]{:S(2)}) %collective-permute-start.1) | collective-permute-done | bytes 81952 | tf_op jit(solution)/shard_map/ppermute | solution.py:170
  6.4 0.0 copy-start.1
  6.5 4.3 %collective-permute-done.lo_ref = f32[5,2,16,128]{3,2,1,0:T(8,128)S(1)} collective-permute-done((f32[5,2,16,128]{3,2,1,0:T(8,128)S(1)}, f32[5,2,16,128]{3,2,1,0:T(8,128)S(1)}, u32[]{:S(2)}, u32[]{:S(2)}) %collective-permute-start) | collective-permute-done | bytes 81952 | tf_op jit(solution)/shard_map/ppermute | solution.py:169
  10.7 0.0 copy-done
  10.7 0.0 copy-done.3
  10.8 0.0 copy-done.4
  10.8 0.0 copy-start.2
  10.8 0.0 copy-done.1
  10.8 0.6 %copy-done.2 = f32[5,2,16,128]{3,2,1,0:T(8,128)} copy-done((f32[5,2,16,128]{3,2,1,0:T(8,128)}, f32[5,2,16,128]{3,2,1,0:T(8,128)S(1)}, u32[]{:S(2)}) %copy-start.2) | copy-done | bytes 81944
  11.4 0.1 collective-permute-start.2
  11.5 1.4 %collective-permute-done.2.side_ref = f32[5,8,8,128]{3,2,1,0:T(8,128)S(1)} collective-permute-done((f32[5,8,8,128]{3,2,1,0:T(8,128)S(1)}, f32[5,8,8,128]{3,2,1,0:T(8,128)S(1)}, u32[]{:S(2)}, u32[]{:S(2)}) %collective-permute-start.2) | collective-permute-done | bytes 163872 | tf_op jit(solution)/shard_map/ppermute | solution.py:173
  12.9 0.0 copy-start.5
  12.9 0.7 %copy-done.5 = f32[5,8,8,128]{3,2,1,0:T(8,128)} copy-done((f32[5,8,8,128]{3,2,1,0:T(8,128)}, f32[5,8,8,128]{3,2,1,0:T(8,128)S(1)}, u32[]{:S(2)}) %copy-start.5) | copy-done | bytes 163864
  13.6 2.2 %stencil.1 = f32[320,128]{1,0:T(8,128)} custom-call(f32[4,16,128]{2,1,0:T(8,128)} %rho_ref.1, f32[4,16,128]{2,1,0:T(8,128)} %en_ref.1, f32[3,4,16,128]{3,2,1,0:T(8,128)} %vel_ref.1, f32[5,2,16,128]{3,2,1,0:T(8,128)} %copy-done.2, f32[5,2,16,128]{3,2,1,0:T(8,128)} %copy-done.1, f32[5,8,8,128]{3,2,1,0:T(8,128)} %copy-done.5), custom_call_target="tpu_custom_call" | custom-call | tf_op jit(solution)/shard_map/stencil/pallas_call | solution.py:175
  15.7 22.8 %all_to_all.18 = f32[32,1280,1]{1,2,0:T(1,128)} all-to-all(f32[32,1280,1]{1,2,0:T(1,128)} %bitcast.6), channel_id=1, replica_groups=mesh['phi'=32,'row'=2,'theta'=4] {'phi'}, dimensions={0} | all-to-all | bytes 327680 | tf_op jit(solution)/shard_map/all_to_all | solution.py:184
  38.5 1.8 %rotate.1 = f32[320,128]{1,0:T(8,128)} custom-call(s32[16]{0:T(128)} %shift_ref.1, f32[16]{0:T(128)} %visc_ref.1, f32[320,128]{1,0:T(8,128)} %bitcast.8), custom_call_target="tpu_custom_call" | custom-call | tf_op jit(solution)/shard_map/rotate/pallas_call | solution.py:187
  40.3 15.5 %all_to_all.19 = f32[32,1280,1]{1,2,0:T(1,128)} all-to-all(f32[32,1280,1]{1,2,0:T(1,128)} %bitcast.9), channel_id=1, replica_groups=mesh['phi'=32,'row'=2,'theta'=4] {'phi'}, dimensions={0} | all-to-all | bytes 327680 | tf_op jit(solution)/shard_map/all_to_all | solution.py:184
  55.8 1.6 %unpack.1 = (f32[4,16,128]{2,1,0:T(8,128)}, f32[4,16,128]{2,1,0:T(8,128)}, f32[3,4,16,128]{3,2,1,0:T(8,128)}) custom-call(f32[320,128]{1,0:T(8,128)} %bitcast.7), custom_call_target="tpu_custom_call" | custom-call | tf_op jit(solution)/shard_map/unpack/pallas_call | solution.py:196
  (3 shorter events, 0.1 us)
Async XLA Ops:
  1.6 9.2 %copy-start = (f32[3,4,16,128]{3,2,1,0:T(8,128)S(1)}, f32[3,4,16,128]{3,2,1,0:T(8,128)}, u32[]{:S(2)}) copy-start(f32[3,4,16,128]{3,2,1,0:T(8,128)} %vel_ref.1) | copy-start | bytes 294916
  1.6 9.2 %copy-start.3 = (f32[4,16,128]{2,1,0:T(8,128)S(1)}, f32[4,16,128]{2,1,0:T(8,128)}, u32[]{:S(2)}) copy-start(f32[4,16,128]{2,1,0:T(8,128)} %rho_ref.1) | copy-start | bytes 98308
  1.6 9.2 %copy-start.4 = (f32[4,16,128]{2,1,0:T(8,128)S(1)}, f32[4,16,128]{2,1,0:T(8,128)}, u32[]{:S(2)}) copy-start(f32[4,16,128]{2,1,0:T(8,128)} %en_ref.1) | copy-start | bytes 98308
  1.6 4.8 %collective-permute-start.1 = (f32[5,2,16,128]{3,2,1,0:T(8,128)S(1)}, f32[5,2,16,128]{3,2,1,0:T(8,128)S(1)}, u32[]{:S(2)}, u32[]{:S(2)}) collective-permute-start(f32[5,2,16,128]{3,2,1,0:T(8,128)S(1)} %get-tuple-element.3), channel_id=1, source_target_pairs={{1,0},{2,1},{3,2},{5,4},{6,5},{7,6},{9,8},{10,9},{11,10},{13,12},{... | collective-permute-start | bytes 245768 | tf_op jit(solution)/shard_map/ppermute | solution.py:170
  4.4 6.3 %collective-permute-start = (f32[5,2,16,128]{3,2,1,0:T(8,128)S(1)}, f32[5,2,16,128]{3,2,1,0:T(8,128)S(1)}, u32[]{:S(2)}, u32[]{:S(2)}) collective-permute-start(f32[5,2,16,128]{3,2,1,0:T(8,128)S(1)} %get-tuple-element.4), channel_id=1, source_target_pairs={{0,1},{1,2},{2,3},{4,5},{5,6},{6,7},{8,9},{9,10},{10,11},{12,13},{... | collective-permute-start | bytes 245768 | tf_op jit(solution)/shard_map/ppermute | solution.py:169
  6.4 4.4 %copy-start.1 = (f32[5,2,16,128]{3,2,1,0:T(8,128)}, f32[5,2,16,128]{3,2,1,0:T(8,128)S(1)}, u32[]{:S(2)}) copy-start(f32[5,2,16,128]{3,2,1,0:T(8,128)S(1)} %collective-permute-done.1.hi_ref) | copy-start | bytes 245764
  10.8 0.6 %copy-start.2 = (f32[5,2,16,128]{3,2,1,0:T(8,128)}, f32[5,2,16,128]{3,2,1,0:T(8,128)S(1)}, u32[]{:S(2)}) copy-start(f32[5,2,16,128]{3,2,1,0:T(8,128)S(1)} %collective-permute-done.lo_ref) | copy-start | bytes 245764
  11.4 1.5 %collective-permute-start.2 = (f32[5,8,8,128]{3,2,1,0:T(8,128)S(1)}, f32[5,8,8,128]{3,2,1,0:T(8,128)S(1)}, u32[]{:S(2)}, u32[]{:S(2)}) collective-permute-start(f32[5,8,8,128]{3,2,1,0:T(8,128)S(1)} %slice_select_fusion), channel_id=1, source_target_pairs={{0,4},{4,0},{1,5},{5,1},{2,6},{6,2},{3,7},{7,3},{8,12},{12,8},{9,1... | collective-permute-start | bytes 491528 | tf_op jit(solution)/shard_map/ppermute | solution.py:173
  12.9 0.7 %copy-start.5 = (f32[5,8,8,128]{3,2,1,0:T(8,128)}, f32[5,8,8,128]{3,2,1,0:T(8,128)S(1)}, u32[]{:S(2)}) copy-start(f32[5,8,8,128]{3,2,1,0:T(8,128)S(1)} %collective-permute-done.2.side_ref) | copy-start | bytes 491524

commit v2 on v1

--- a/solution.py
+++ b/solution.py
@@ -56,7 +56,7 @@
     return d_rho, d_en, d_vr, d_vt, d_vp
 
 
-def stencil_kernel(rho_ref, en_ref, vel_ref, lo_ref, hi_ref, side_ref, out_ref):
+def stencil_kernel(own_ref, lo_ref, hi_ref, side_ref, out_ref):
     row = lax.axis_index("row")
     theta = lax.axis_index("theta")
     pos = lax.broadcasted_iota(jnp.int32, (TILE, LANES), 0)
@@ -67,8 +67,7 @@
             return lo_ref[f, t]
         if t >= TH + 2:
             return hi_ref[f, t - TH - 2]
-        t -= 2
-        return rho_ref[t] if f == 0 else en_ref[t] if f == 1 else vel_ref[f - 2, t]
+        return own_ref[f, t - 2]
 
     def wide(f, t):
         return jnp.concatenate([own(f, t), jnp.where(near, side_ref[f, t], 0.0)], 0)
@@ -160,6 +159,10 @@
     return pl.BlockSpec(memory_space=pltpu.SMEM)
 
 
+def near(value):
+    return pltpu.with_memory_space_constraint(value, pltpu.VMEM)
+
+
 def per_device(density, energy, velocity, shifts, viscosity):
     thetas = lax.axis_size("theta")
     rows = lax.axis_index("row")
@@ -171,14 +174,14 @@
     tall = jnp.concatenate([lo, fields, hi], 1)
     edge = jnp.where(rows == 0, tall[:, :, CR - TILE :], tall[:, :, :TILE])
     side = lax.ppermute(edge, "row", [(0, 1), (1, 0)])
-    flat = jax.ShapeDtypeStruct((PHI * ROWS, LANES), jnp.float32)
+    flat = pltpu.VMEM((PHI * ROWS, LANES), jnp.float32)
     second = pl.pallas_call(
         stencil_kernel,
         out_shape=flat,
-        in_specs=[vmem()] * 6,
+        in_specs=[vmem()] * 4,
         out_specs=vmem(),
         name="stencil",
-    )(density, energy, velocity, lo, hi, side)
+    )(near(fields), near(lo), near(hi), near(side))
 
     def exchange(value):
         value = lax.all_to_all(value.reshape(-1), "phi", 0, 0, tiled=True)
@@ -191,7 +194,7 @@
         out_specs=vmem(),
         scratch_shapes=[pltpu.VMEM((ROWS, 2 * PHI, LANES), jnp.float32)],
         name="rotate",
-    )(shifts, viscosity, exchange(second))
+    )(shifts, viscosity, near(exchange(second)))
     block = jax.ShapeDtypeStruct(density.shape, jnp.float32)
     return pl.pallas_call(
         unpack_kernel,
@@ -199,7 +202,7 @@
         in_specs=[vmem()],
         out_specs=(vmem(), vmem(), vmem()),
         name="unpack",
-    )(exchange(turned))
+    )(near(exchange(turned)))
 
 
 def solution(mesh):

time: 57.8 us -> 51.4 us (0.89)
  Pallas kernels: 5.59 us -> 2.03 us
  blocking collectives: 38.3 us -> 36.8 us
  local copies, waits for them, and re-layouts: 1.28 us -> 0.03 us
    pallas_call x1, Pallas kernels: 2.17 us -> 0.44 us  [per_device(): pl.pallas_call(stencil_kernel, out_shape=flat, in_specs=[vmem()] * 4, out...]
    all_to_all x2, blocking collectives: 38.3 us -> 36.8 us  [exchange(): value = lax.all_to_all(value.reshape(-1), 'phi', 0, 0, tiled=True)]
    unnamed x12 -> x6, local copies, waits for them, and re-layouts: 1.26 us -> 0.02 us
    pallas_call x1, Pallas kernels: 1.59 us -> 0.67 us  [per_device(): pl.pallas_call(unpack_kernel, out_shape=(block, block, jax.ShapeDtypeStru...]
    pallas_call x1, Pallas kernels: 1.83 us -> 0.92 us  [per_device(): pl.pallas_call(rotate_kernel, out_shape=flat, in_specs=[smem(), smem(), v...]
where the time goes in v2:
time: 51.4 us; the launch traced here: 51.1 us
  blocking collectives  36.8 us (72%)
  waiting for transfers between devices  6.41 us (12%)
  starting transfers between devices  4.17 us (8%)
  Pallas kernels  2.03 us (4%)
  other arithmetic  0.98 us (2%)
  between operations  0.72 us (1%)
    all_to_all x2, blocking collectives, exchange(): value = lax.all_to_all(value.reshape(-1), 'phi', 0, 0, tiled=True)  36.8 us
    ppermute x1, waiting for transfers between devices, per_device(): lo = lax.ppermute(fields[:, TH - 2:], 'theta', upward)  4.3 us
    ppermute x1, starting transfers between devices, per_device(): hi = lax.ppermute(fields[:, :2], 'theta', downward)  2.78 us
    ppermute x1, waiting for transfers between devices, per_device(): side = lax.ppermute(edge, 'row', [(0, 1), (1, 0)])  1.38 us
    ppermute x1, starting transfers between devices, per_device(): lo = lax.ppermute(fields[:, TH - 2:], 'theta', upward)  1.29 us
  transfers between devices with their start and end apart: 3, of which 3 were waited for; matrix products, arithmetic and copies ran while one was open for 0% of the time, Pallas kernels for 0%

profile of v2, /device:TPU:24, one launch (start us, length us, event | category | flops | bytes accessed | tf_op | source)
XLA Modules:
  0.0 51.1 jit_solution(12245757281117898721)
XLA Ops:
  0.6 0.9 %pad_maximum_fusion.1.own_ref = f32[5,4,16,128]{3,2,1,0:T(8,128)S(1)} fusion(f32[3,4,16,128]{3,2,1,0:T(8,128)} %param.7, f32[1,4,16,128]{3,2,1,0:T(8,128)} %bitcast.10, f32[1,4,16,128]{3,2,1,0:T(8,128)} %bitcast.12), kind=kLoop, calls=%fused_computation.2 | loop fusion | flops 81920 | bytes 327680 | tf_op jit(solution)/shard_map/concatenate | solution.py:169
  1.6 0.0 copy-start
  1.6 0.0 copy-start.1
  1.6 0.0 copy-start.2
  1.6 2.8 %collective-permute-start.1 = (f32[5,2,16,128]{3,2,1,0:T(8,128)S(1)}, f32[5,2,16,128]{3,2,1,0:T(8,128)S(1)}, u32[]{:S(2)}, u32[]{:S(2)}) collective-permute-start(f32[5,2,16,128]{3,2,1,0:T(8,128)S(1)} %get-tuple-element.3), channel_id=1, source_target_pairs={{1,0},{2,1},{3,2},{5,4},{6,5},{7,6},{9,8},{10,9},{11,10},{13,12},{... | collective-permute-start | bytes 245768 | tf_op jit(solution)/shard_map/ppermute | solution.py:173
  4.4 1.3 %collective-permute-start = (f32[5,2,16,128]{3,2,1,0:T(8,128)S(1)}, f32[5,2,16,128]{3,2,1,0:T(8,128)S(1)}, u32[]{:S(2)}, u32[]{:S(2)}) collective-permute-start(f32[5,2,16,128]{3,2,1,0:T(8,128)S(1)} %get-tuple-element.4), channel_id=1, source_target_pairs={{0,1},{1,2},{2,3},{4,5},{5,6},{6,7},{8,9},{9,10},{10,11},{12,13},{... | collective-permute-start | bytes 245768 | tf_op jit(solution)/shard_map/ppermute | solution.py:172
  5.7 0.7 %collective-permute-done.1.hi_ref = f32[5,2,16,128]{3,2,1,0:T(8,128)S(1)} collective-permute-done((f32[5,2,16,128]{3,2,1,0:T(8,128)S(1)}, f32[5,2,16,128]{3,2,1,0:T(8,128)S(1)}, u32[]{:S(2)}, u32[]{:S(2)}) %collective-permute-start.1) | collective-permute-done | bytes 81952 | tf_op jit(solution)/shard_map/ppermute | solution.py:173
  6.4 4.3 %collective-permute-done.lo_ref = f32[5,2,16,128]{3,2,1,0:T(8,128)S(1)} collective-permute-done((f32[5,2,16,128]{3,2,1,0:T(8,128)S(1)}, f32[5,2,16,128]{3,2,1,0:T(8,128)S(1)}, u32[]{:S(2)}, u32[]{:S(2)}) %collective-permute-start) | collective-permute-done | bytes 81952 | tf_op jit(solution)/shard_map/ppermute | solution.py:172
  10.7 0.0 copy-done
  10.7 0.0 copy-done.1
  10.8 0.0 copy-done.2
  10.8 0.1 collective-permute-start.2
  10.9 1.4 %collective-permute-done.2.side_ref = f32[5,8,8,128]{3,2,1,0:T(8,128)S(1)} collective-permute-done((f32[5,8,8,128]{3,2,1,0:T(8,128)S(1)}, f32[5,8,8,128]{3,2,1,0:T(8,128)S(1)}, u32[]{:S(2)}, u32[]{:S(2)}) %collective-permute-start.2) | collective-permute-done | bytes 163872 | tf_op jit(solution)/shard_map/ppermute | solution.py:176
  12.3 0.4 stencil.1
  12.7 22.5 %all_to_all.18 = f32[32,1280,1]{1,2,0:T(1,128)S(1)} all-to-all(f32[32,1280,1]{1,2,0:T(1,128)S(1)} %bitcast.6), channel_id=1, replica_groups=mesh['phi'=32,'row'=2,'theta'=4] {'phi'}, dimensions={0} | all-to-all | bytes 327680 | tf_op jit(solution)/shard_map/all_to_all | solution.py:187
  35.2 0.9 %rotate.1 = f32[320,128]{1,0:T(8,128)S(1)} custom-call(s32[16]{0:T(128)} %shift_ref.1, f32[16]{0:T(128)} %visc_ref.1, f32[320,128]{1,0:T(8,128)S(1)} %bitcast.8), custom_call_target="tpu_custom_call" | custom-call | tf_op jit(solution)/shard_map/rotate/pallas_call | solution.py:190
  36.1 14.3 %all_to_all.19 = f32[32,1280,1]{1,2,0:T(1,128)S(1)} all-to-all(f32[32,1280,1]{1,2,0:T(1,128)S(1)} %bitcast.9), channel_id=1, replica_groups=mesh['phi'=32,'row'=2,'theta'=4] {'phi'}, dimensions={0} | all-to-all | bytes 327680 | tf_op jit(solution)/shard_map/all_to_all | solution.py:187
  50.4 0.7 %unpack.1 = (f32[4,16,128]{2,1,0:T(8,128)}, f32[4,16,128]{2,1,0:T(8,128)}, f32[3,4,16,128]{3,2,1,0:T(8,128)}) custom-call(f32[320,128]{1,0:T(8,128)S(1)} %bitcast.7), custom_call_target="tpu_custom_call" | custom-call | tf_op jit(solution)/shard_map/unpack/pallas_call | solution.py:199
  (3 shorter events, 0.1 us)
Async XLA Ops:
  1.6 9.2 %copy-start = (f32[3,4,16,128]{3,2,1,0:T(8,128)S(1)}, f32[3,4,16,128]{3,2,1,0:T(8,128)}, u32[]{:S(2)}) copy-start(f32[3,4,16,128]{3,2,1,0:T(8,128)} %param.7) | copy-start | bytes 294916
  1.6 9.2 %copy-start.1 = (f32[4,16,128]{2,1,0:T(8,128)S(1)}, f32[4,16,128]{2,1,0:T(8,128)}, u32[]{:S(2)}) copy-start(f32[4,16,128]{2,1,0:T(8,128)} %param.6) | copy-start | bytes 98308
  1.6 9.2 %copy-start.2 = (f32[4,16,128]{2,1,0:T(8,128)S(1)}, f32[4,16,128]{2,1,0:T(8,128)}, u32[]{:S(2)}) copy-start(f32[4,16,128]{2,1,0:T(8,128)} %param.5) | copy-start | bytes 98308
  1.6 4.8 %collective-permute-start.1 = (f32[5,2,16,128]{3,2,1,0:T(8,128)S(1)}, f32[5,2,16,128]{3,2,1,0:T(8,128)S(1)}, u32[]{:S(2)}, u32[]{:S(2)}) collective-permute-start(f32[5,2,16,128]{3,2,1,0:T(8,128)S(1)} %get-tuple-element.3), channel_id=1, source_target_pairs={{1,0},{2,1},{3,2},{5,4},{6,5},{7,6},{9,8},{10,9},{11,10},{13,12},{... | collective-permute-start | bytes 245768 | tf_op jit(solution)/shard_map/ppermute | solution.py:173
  4.4 6.3 %collective-permute-start = (f32[5,2,16,128]{3,2,1,0:T(8,128)S(1)}, f32[5,2,16,128]{3,2,1,0:T(8,128)S(1)}, u32[]{:S(2)}, u32[]{:S(2)}) collective-permute-start(f32[5,2,16,128]{3,2,1,0:T(8,128)S(1)} %get-tuple-element.4), channel_id=1, source_target_pairs={{0,1},{1,2},{2,3},{4,5},{5,6},{6,7},{8,9},{9,10},{10,11},{12,13},{... | collective-permute-start | bytes 245768 | tf_op jit(solution)/shard_map/ppermute | solution.py:172
  10.8 1.5 %collective-permute-start.2 = (f32[5,8,8,128]{3,2,1,0:T(8,128)S(1)}, f32[5,8,8,128]{3,2,1,0:T(8,128)S(1)}, u32[]{:S(2)}, u32[]{:S(2)}) collective-permute-start(f32[5,8,8,128]{3,2,1,0:T(8,128)S(1)} %slice_select_fusion), channel_id=1, source_target_pairs={{0,4},{4,0},{1,5},{5,1},{2,6},{6,2},{3,7},{7,3},{8,12},{12,8},{9,1... | collective-permute-start | bytes 491528 | tf_op jit(solution)/shard_map/ppermute | solution.py:176

commit v3 on v2

--- a/solution.py
+++ b/solution.py
@@ -56,21 +56,43 @@
     return d_rho, d_en, d_vr, d_vt, d_vp
 
 
-def stencil_kernel(own_ref, lo_ref, hi_ref, side_ref, out_ref):
+def pack_kernel(rho_ref, en_ref, vel_ref, shift_ref, visc_ref, out_ref, hop_ref, nu_ref, sems):
+    copies = [
+        pltpu.make_async_copy(shift_ref, hop_ref, sems.at[3]),
+        pltpu.make_async_copy(visc_ref, nu_ref, sems.at[4]),
+        pltpu.make_async_copy(rho_ref, out_ref.at[0], sems.at[0]),
+        pltpu.make_async_copy(en_ref, out_ref.at[1], sems.at[1]),
+        pltpu.make_async_copy(vel_ref, out_ref.at[2:], sems.at[2]),
+    ]
+    for copy in copies:
+        copy.start()
+    for copy in copies:
+        copy.wait()
+
+
+def stencil_kernel(own_ref, sib_ref, got_ref, passed_ref, out_ref):
     row = lax.axis_index("row")
     theta = lax.axis_index("theta")
     pos = lax.broadcasted_iota(jnp.int32, (TILE, LANES), 0)
     near = jnp.where(row == 0, pos, TILE - 1 - pos) < TILE // 2
 
-    def own(f, t):
+    def halo(f, t, low):
+        parts = []
+        for start, size in ((CR * row, CR), (CR - TILE * row, TILE)):
+            span = pl.ds(pl.multiple_of(start, TILE), size)
+            got, passed = got_ref[f, t, span, :], passed_ref[f, t, span, :]
+            parts.append(jnp.where((row == 0) == low, got, passed))
+        return parts
+
+    def wide(f, t):
         if t < 2:
-            return lo_ref[f, t]
-        if t >= TH + 2:
-            return hi_ref[f, t - TH - 2]
-        return own_ref[f, t - 2]
-
-    def wide(f, t):
-        return jnp.concatenate([own(f, t), jnp.where(near, side_ref[f, t], 0.0)], 0)
+            own, side = halo(f, t, True)
+        elif t >= TH + 2:
+            own, side = halo(f, t - TH - 2, False)
+        else:
+            own = own_ref[f, t - 2]
+            side = sib_ref[f, t - 2, pl.ds(pl.multiple_of(TILE * row, TILE), TILE), :]
+        return jnp.concatenate([own, jnp.where(near, side, 0.0)], 0)
 
     field = [[wide(f, t) for t in range(TH + 4)] for f in range(FIELDS)]
     first = [[None] * (TH + 4) for _ in range(FIELDS)]
@@ -165,15 +187,36 @@
 
 def per_device(density, energy, velocity, shifts, viscosity):
     thetas = lax.axis_size("theta")
-    rows = lax.axis_index("row")
-    fields = jnp.concatenate([density[None], energy[None], velocity], 0)
-    upward = [(i, i + 1) for i in range(thetas - 1)]
-    downward = [(j, i) for i, j in upward]
-    lo = lax.ppermute(fields[:, TH - 2 :], "theta", upward)
-    hi = lax.ppermute(fields[:, :2], "theta", downward)
-    tall = jnp.concatenate([lo, fields, hi], 1)
-    edge = jnp.where(rows == 0, tall[:, :, CR - TILE :], tall[:, :, :TILE])
-    side = lax.ppermute(edge, "row", [(0, 1), (1, 0)])
+    row = lax.axis_index("row")
+    swap = [(0, 1), (1, 0)]
+    sibling = jnp.concatenate(
+        [
+            lax.ppermute(density, "row", swap)[None],
+            lax.ppermute(energy, "row", swap)[None],
+            lax.ppermute(velocity, "row", swap),
+        ],
+        0,
+    )
+    fields, hops, nu = pl.pallas_call(
+        pack_kernel,
+        out_shape=(
+            pltpu.VMEM((FIELDS,) + density.shape, jnp.float32),
+            pltpu.SMEM(shifts.shape, jnp.int32),
+            pltpu.SMEM(viscosity.shape, jnp.float32),
+        ),
+        in_specs=[pl.BlockSpec(memory_space=pl.ANY)] * 5,
+        out_specs=(vmem(), smem(), smem()),
+        scratch_shapes=[pltpu.SemaphoreType.DMA((5,))],
+        name="pack",
+    )(density, energy, velocity, shifts, viscosity)
+    outer = jnp.where(
+        row == 0,
+        jnp.concatenate([fields[:, :2], sibling[:, :2]], 2),
+        jnp.concatenate([sibling[:, TH - 2 :], fields[:, TH - 2 :]], 2),
+    )
+    across = [(thetas + i, i + 1) for i in range(thetas - 1)]
+    got = lax.ppermute(outer, ("row", "theta"), across + [(j, i) for i, j in across])
+    passed = lax.ppermute(got, "row", swap)
     flat = pltpu.VMEM((PHI * ROWS, LANES), jnp.float32)
     second = pl.pallas_call(
         stencil_kernel,
@@ -181,7 +224,7 @@
         in_specs=[vmem()] * 4,
         out_specs=vmem(),
         name="stencil",
-    )(near(fields), near(lo), near(hi), near(side))
+    )(near(fields), near(sibling), near(got), near(passed))
 
     def exchange(value):
         value = lax.all_to_all(value.reshape(-1), "phi", 0, 0, tiled=True)
@@ -194,7 +237,11 @@
         out_specs=vmem(),
         scratch_shapes=[pltpu.VMEM((ROWS, 2 * PHI, LANES), jnp.float32)],
         name="rotate",
-    )(shifts, viscosity, near(exchange(second)))
+    )(
+        pltpu.with_memory_space_constraint(hops, pltpu.SMEM),
+        pltpu.with_memory_space_constraint(nu, pltpu.SMEM),
+        near(exchange(second)),
+    )
     block = jax.ShapeDtypeStruct(density.shape, jnp.float32)
     return pl.pallas_call(
         unpack_kernel,

time: 51.4 us -> 49.2 us (0.957)
  starting transfers between devices: 4.17 us -> 3.1 us
  other arithmetic: 0.98 us -> 0.04 us
    ppermute x3 -> x5, starting transfers between devices: 4.17 us -> 3.1 us  [the longest x1 2.41 us: per_device(): lax.ppermute(outer, ('row', 'theta'), across + [(j, i) for i, j in across])]
    pallas_call x0 -> x1, Pallas kernels: none -> 0.98 us  [per_device(): pl.pallas_call(pack_kernel, out_shape=(pltpu.VMEM((FIELDS,) + density.sha...]
    concatenate x2 -> x1, other arithmetic: 0.95 us -> 0.01 us  [per_device(): jnp.concatenate([lax.ppermute(density, 'row', swap)[None], lax.ppermute(e...]
    pallas_call x1, Pallas kernels: 0.92 us -> 0.24 us  [per_device(): pl.pallas_call(rotate_kernel, out_shape=flat, in_specs=[smem(), smem(), v...]
    ppermute x3 -> x5, waiting for transfers between devices: 6.41 us -> 6 us  [the longest x1 4.22 us: per_device(): lax.ppermute(outer, ('row', 'theta'), across + [(j, i) for i, j in across])]
  transfers between devices with their start and end apart: 3 -> 5, of which waited for: 3 -> 3; matrix products, arithmetic and copies ran while one was open for 0% -> 0% of each run, Pallas kernels for 0% -> 2%
where the time goes in v3:
time: 49.2 us; the launch traced here: 49 us
  blocking collectives  36.8 us (75%)
  waiting for transfers between devices  6 us (12%)
  starting transfers between devices  3.1 us (6%)
  Pallas kernels  2.34 us (5%)
  between operations  0.72 us (1%)
    all_to_all x2, blocking collectives, exchange(): value = lax.all_to_all(value.reshape(-1), 'phi', 0, 0, tiled=True)  36.8 us
    ppermute x1, waiting for transfers between devices, per_device(): lax.ppermute(outer, ('row', 'theta'), across + [(j, i) for i, j in across])  4.22 us
    ppermute x1, starting transfers between devices, per_device(): lax.ppermute(outer, ('row', 'theta'), across + [(j, i) for i, j in across])  2.41 us
    ppermute x1, waiting for transfers between devices, per_device(): passed = lax.ppermute(got, 'row', swap)  1.39 us
  transfers between devices with their start and end apart: 5, of which 3 were waited for; matrix products, arithmetic and copies ran while one was open for 0% of the time, Pallas kernels for 2%

profile of v3, /device:TPU:24, one launch (start us, length us, event | category | flops | bytes accessed | tf_op | source)
XLA Modules:
  0.0 49.0 jit_solution(6970883021837255951)
XLA Ops:
  0.6 0.1 collective-permute-start
  0.7 0.5 %collective-permute-start.1 = (f32[4,16,128]{2,1,0:T(8,128)}, f32[4,16,128]{2,1,0:T(8,128)S(1)}, u32[]{:S(2)}, u32[]{:S(2)}) collective-permute-start(f32[4,16,128]{2,1,0:T(8,128)} %en_ref.1), channel_id=1, source_target_pairs={{0,4},{4,0},{1,5},{5,1},{2,6},{6,2},{3,7},{7,3},{8,12},{12,8},{9,1... | collective-permute-start | bytes 98312 | tf_op jit(solution)/shard_map/ppermute | solution.py:195
  1.2 0.1 collective-permute-start.2
  1.3 1.0 %pack.1 = (f32[5,4,16,128]{3,2,1,0:T(8,128)S(1)}, s32[16]{0:T(128)S(4)}, f32[16]{0:T(128)S(4)}) custom-call(f32[4,16,128]{2,1,0:T(8,128)} %rho_ref.1, f32[4,16,128]{2,1,0:T(8,128)} %en_ref.1, f32[3,4,16,128]{3,2,1,0:T(8,128)} %vel_ref.1, s32[16]{0:T(128)} %shift_ref.1, f32[16]{0:T(128)} %visc_ref.1), custom_call_target="tpu_custom_call" | custom-call | tf_op jit(solution)/shard_map/pack/pallas_call | solution.py:200
  2.3 0.0 collective-permute-done
  2.4 0.0 collective-permute-done.1
  2.4 0.4 collective-permute-done.2
  2.8 2.4 %collective-permute-start.3 = (f32[5,2,32,128]{3,2,1,0:T(8,128)S(1)}, f32[5,2,32,128]{3,2,1,0:T(8,128)S(1)}, u32[]{:S(2)}, u32[]{:S(2)}) collective-permute-start(f32[5,2,32,128]{3,2,1,0:T(8,128)S(1)} %maximum_select_fusion), channel_id=1, source_target_pairs={{4,1},{5,2},{6,3},{1,4},{2,5},{3,6},{12,9},{13,10},{14,11},{9,12},... | collective-permute-start | bytes 491528 | tf_op jit(solution)/shard_map/ppermute | solution.py:218
  5.2 4.2 %collective-permute-done.3.got_ref = f32[5,2,32,128]{3,2,1,0:T(8,128)S(1)} collective-permute-done((f32[5,2,32,128]{3,2,1,0:T(8,128)S(1)}, f32[5,2,32,128]{3,2,1,0:T(8,128)S(1)}, u32[]{:S(2)}, u32[]{:S(2)}) %collective-permute-start.3) | collective-permute-done | bytes 163872 | tf_op jit(solution)/shard_map/ppermute | solution.py:218
  9.4 0.0 collective-permute-start.4
  9.5 1.4 %collective-permute-done.4.passed_ref = f32[5,2,32,128]{3,2,1,0:T(8,128)S(1)} collective-permute-done((f32[5,2,32,128]{3,2,1,0:T(8,128)S(1)}, f32[5,2,32,128]{3,2,1,0:T(8,128)S(1)}, u32[]{:S(2)}, u32[]{:S(2)}) %collective-permute-start.4) | collective-permute-done | bytes 163872 | tf_op jit(solution)/shard_map/ppermute | solution.py:219
  10.8 0.5 stencil.1
  11.3 22.5 %all_to_all.18 = f32[32,1280,1]{1,2,0:T(1,128)S(1)} all-to-all(f32[32,1280,1]{1,2,0:T(1,128)S(1)} %bitcast.9), channel_id=1, replica_groups=mesh['phi'=32,'row'=2,'theta'=4] {'phi'}, dimensions={0} | all-to-all | bytes 327680 | tf_op jit(solution)/shard_map/all_to_all | solution.py:230
  33.8 0.2 rotate.1
  34.0 14.3 %all_to_all.19 = f32[32,1280,1]{1,2,0:T(1,128)S(1)} all-to-all(f32[32,1280,1]{1,2,0:T(1,128)S(1)} %bitcast.8), channel_id=1, replica_groups=mesh['phi'=32,'row'=2,'theta'=4] {'phi'}, dimensions={0} | all-to-all | bytes 327680 | tf_op jit(solution)/shard_map/all_to_all | solution.py:230
  48.3 0.7 %unpack.1 = (f32[4,16,128]{2,1,0:T(8,128)}, f32[4,16,128]{2,1,0:T(8,128)}, f32[3,4,16,128]{3,2,1,0:T(8,128)}) custom-call(f32[320,128]{1,0:T(8,128)S(1)} %bitcast.7), custom_call_target="tpu_custom_call" | custom-call | tf_op jit(solution)/shard_map/unpack/pallas_call | solution.py:246
  (4 shorter events, 0.1 us)
Async XLA Ops:
  0.6 1.7 %collective-permute-start = (f32[4,16,128]{2,1,0:T(8,128)}, f32[4,16,128]{2,1,0:T(8,128)S(1)}, u32[]{:S(2)}, u32[]{:S(2)}) collective-permute-start(f32[4,16,128]{2,1,0:T(8,128)} %rho_ref.1), channel_id=1, source_target_pairs={{0,4},{4,0},{1,5},{5,1},{2,6},{6,2},{3,7},{7,3},{8,12},{12,8},{9,1... | collective-permute-start | bytes 98312 | tf_op jit(solution)/shard_map/ppermute | solution.py:194
  0.7 1.6 %collective-permute-start.1 = (f32[4,16,128]{2,1,0:T(8,128)}, f32[4,16,128]{2,1,0:T(8,128)S(1)}, u32[]{:S(2)}, u32[]{:S(2)}) collective-permute-start(f32[4,16,128]{2,1,0:T(8,128)} %en_ref.1), channel_id=1, source_target_pairs={{0,4},{4,0},{1,5},{5,1},{2,6},{6,2},{3,7},{7,3},{8,12},{12,8},{9,1... | collective-permute-start | bytes 98312 | tf_op jit(solution)/shard_map/ppermute | solution.py:195
  1.2 1.5 %collective-permute-start.2 = (f32[3,4,16,128]{3,2,1,0:T(8,128)}, f32[3,4,16,128]{3,2,1,0:T(8,128)S(1)}, u32[]{:S(2)}, u32[]{:S(2)}) collective-permute-start(f32[3,4,16,128]{3,2,1,0:T(8,128)} %vel_ref.1), channel_id=1, source_target_pairs={{0,4},{4,0},{1,5},{5,1},{2,6},{6,2},{3,7},{7,3},{8,12},{12,8},{9,1... | collective-permute-start | bytes 294920 | tf_op jit(solution)/shard_map/ppermute | solution.py:196
  2.8 6.6 %collective-permute-start.3 = (f32[5,2,32,128]{3,2,1,0:T(8,128)S(1)}, f32[5,2,32,128]{3,2,1,0:T(8,128)S(1)}, u32[]{:S(2)}, u32[]{:S(2)}) collective-permute-start(f32[5,2,32,128]{3,2,1,0:T(8,128)S(1)} %maximum_select_fusion), channel_id=1, source_target_pairs={{4,1},{5,2},{6,3},{1,4},{2,5},{3,6},{12,9},{13,10},{14,11},{9,12},... | collective-permute-start | bytes 491528 | tf_op jit(solution)/shard_map/ppermute | solution.py:218
  9.4 1.4 %collective-permute-start.4 = (f32[5,2,32,128]{3,2,1,0:T(8,128)S(1)}, f32[5,2,32,128]{3,2,1,0:T(8,128)S(1)}, u32[]{:S(2)}, u32[]{:S(2)}) collective-permute-start(f32[5,2,32,128]{3,2,1,0:T(8,128)S(1)} %collective-permute-done.3.got_ref), channel_id=1, source_target_pairs={{0,4},{4,0},{1,5},{5,1},{2,6},{6,2},{3,7},{7,3},{8,12},{12,8},{9,1... | collective-permute-start | bytes 491528 | tf_op jit(solution)/shard_map/ppermute | solution.py:219

commit v4 on v3

--- a/solution.py
+++ b/solution.py
@@ -84,26 +84,25 @@
             parts.append(jnp.where((row == 0) == low, got, passed))
         return parts
 
+    near = jnp.concatenate([jnp.ones((CR, LANES), jnp.bool_), near], 0)
+    below = near & (theta > 0)
+    above = near & (theta < lax.axis_size("theta") - 1)
+
     def wide(f, t):
         if t < 2:
-            own, side = halo(f, t, True)
+            inside, parts = below, halo(f, t, True)
         elif t >= TH + 2:
-            own, side = halo(f, t - TH - 2, False)
+            inside, parts = above, halo(f, t - TH - 2, False)
         else:
-            own = own_ref[f, t - 2]
             side = sib_ref[f, t - 2, pl.ds(pl.multiple_of(TILE * row, TILE), TILE), :]
-        return jnp.concatenate([own, jnp.where(near, side, 0.0)], 0)
+            inside, parts = near, [own_ref[f, t - 2], side]
+        return jnp.where(inside, jnp.concatenate(parts, 0), 0.0)
 
     field = [[wide(f, t) for t in range(TH + 4)] for f in range(FIELDS)]
     first = [[None] * (TH + 4) for _ in range(FIELDS)]
-    side_in = jnp.concatenate([jnp.ones((CR, LANES), jnp.bool_), near], 0)
     inverse = [None] * (TH + 4)
     for t in range(1, TH + 3):
-        inside = side_in
-        if t == 1:
-            inside = side_in & (theta > 0)
-        if t == TH + 2:
-            inside = side_in & (theta < lax.axis_size("theta") - 1)
+        inside = below if t == 1 else above if t == TH + 2 else near
         inverse[t] = 1.0 / jnp.where(inside, field[0][t], 1.0)
         steps = rates(field, inverse[t], t)
         for f in range(FIELDS):
@@ -214,7 +213,7 @@
         jnp.concatenate([fields[:, :2], sibling[:, :2]], 2),
         jnp.concatenate([sibling[:, TH - 2 :], fields[:, TH - 2 :]], 2),
     )
-    across = [(thetas + i, i + 1) for i in range(thetas - 1)]
+    across = [(thetas + i, (i + 1) % thetas) for i in range(thetas)]
     got = lax.ppermute(outer, ("row", "theta"), across + [(j, i) for i, j in across])
     passed = lax.ppermute(got, "row", swap)
     flat = pltpu.VMEM((PHI * ROWS, LANES), jnp.float32)

time: 49.2 us -> 48.5 us (0.986)
    ppermute x1, starting transfers between devices: 2.41 us -> 0.59 us  [per_device(): lax.ppermute(outer, ('row', 'theta'), across + [(j, i) for i, j in across])]
    ppermute x1, starting transfers between devices: 0.01 us -> 1.36 us  [per_device(): passed = lax.ppermute(got, 'row', swap)]
where the time goes in v4:
time: 48.5 us; the launch traced here: 48.4 us
  blocking collectives  36.9 us (76%)
  waiting for transfers between devices  5.66 us (12%)
  starting transfers between devices  2.64 us (5%)
  Pallas kernels  2.35 us (5%)
  between operations  0.71 us (1%)
    all_to_all x2, blocking collectives, exchange(): value = lax.all_to_all(value.reshape(-1), 'phi', 0, 0, tiled=True)  36.9 us
    ppermute x1, waiting for transfers between devices, per_device(): lax.ppermute(outer, ('row', 'theta'), across + [(j, i) for i, j in across])  4.24 us
    ppermute x1, starting transfers between devices, per_device(): passed = lax.ppermute(got, 'row', swap)  1.36 us
    ppermute x1, waiting for transfers between devices, per_device(): passed = lax.ppermute(got, 'row', swap)  1.03 us
    pallas_call x1, Pallas kernels, per_device(): pl.pallas_call(pack_kernel, out_shape=(pltpu.VMEM((FIELDS,) + density.sha...  0.98 us
  transfers between devices with their start and end apart: 5, of which 3 were waited for; matrix products, arithmetic and copies ran while one was open for 0% of the time, Pallas kernels for 2%

profile of v4, /device:TPU:24, one launch (start us, length us, event | category | flops | bytes accessed | tf_op | source)
XLA Modules:
  0.0 48.4 jit_solution(8409776317391920470)
XLA Ops:
  0.6 0.1 collective-permute-start
  0.7 0.5 %collective-permute-start.1 = (f32[4,16,128]{2,1,0:T(8,128)}, f32[4,16,128]{2,1,0:T(8,128)S(1)}, u32[]{:S(2)}, u32[]{:S(2)}) collective-permute-start(f32[4,16,128]{2,1,0:T(8,128)} %en_ref.1), channel_id=1, source_target_pairs={{0,4},{4,0},{1,5},{5,1},{2,6},{6,2},{3,7},{7,3},{8,12},{12,8},{9,1... | collective-permute-start | bytes 98312 | tf_op jit(solution)/shard_map/ppermute | solution.py:194
  1.2 0.1 collective-permute-start.2
  1.3 1.0 %pack.1 = (f32[5,4,16,128]{3,2,1,0:T(8,128)S(1)}, s32[16]{0:T(128)S(4)}, f32[16]{0:T(128)S(4)}) custom-call(f32[4,16,128]{2,1,0:T(8,128)} %rho_ref.1, f32[4,16,128]{2,1,0:T(8,128)} %en_ref.1, f32[3,4,16,128]{3,2,1,0:T(8,128)} %vel_ref.1, s32[16]{0:T(128)} %shift_ref.1, f32[16]{0:T(128)} %visc_ref.1), custom_call_target="tpu_custom_call" | custom-call | tf_op jit(solution)/shard_map/pack/pallas_call | solution.py:199
  2.3 0.0 collective-permute-done
  2.4 0.0 collective-permute-done.1
  2.4 0.4 collective-permute-done.2
  2.8 0.6 %collective-permute-start.3 = (f32[5,2,32,128]{3,2,1,0:T(8,128)S(1)}, f32[5,2,32,128]{3,2,1,0:T(8,128)S(1)}, u32[]{:S(2)}, u32[]{:S(2)}) collective-permute-start(f32[5,2,32,128]{3,2,1,0:T(8,128)S(1)} %maximum_select_fusion), channel_id=1, source_target_pairs={{4,1},{5,2},{6,3},{7,0},{1,4},{2,5},{3,6},{0,7},{12,9},{13,10},{14... | collective-permute-start | bytes 491528 | tf_op jit(solution)/shard_map/ppermute | solution.py:217
  3.4 4.2 %collective-permute-done.3.got_ref = f32[5,2,32,128]{3,2,1,0:T(8,128)S(1)} collective-permute-done((f32[5,2,32,128]{3,2,1,0:T(8,128)S(1)}, f32[5,2,32,128]{3,2,1,0:T(8,128)S(1)}, u32[]{:S(2)}, u32[]{:S(2)}) %collective-permute-start.3) | collective-permute-done | bytes 163872 | tf_op jit(solution)/shard_map/ppermute | solution.py:217
  7.6 1.4 %collective-permute-start.4 = (f32[5,2,32,128]{3,2,1,0:T(8,128)S(1)}, f32[5,2,32,128]{3,2,1,0:T(8,128)S(1)}, u32[]{:S(2)}, u32[]{:S(2)}) collective-permute-start(f32[5,2,32,128]{3,2,1,0:T(8,128)S(1)} %collective-permute-done.3.got_ref), channel_id=1, source_target_pairs={{0,4},{4,0},{1,5},{5,1},{2,6},{6,2},{3,7},{7,3},{8,12},{12,8},{9,1... | collective-permute-start | bytes 491528 | tf_op jit(solution)/shard_map/ppermute | solution.py:218
  9.0 1.0 %collective-permute-done.4.passed_ref = f32[5,2,32,128]{3,2,1,0:T(8,128)S(1)} collective-permute-done((f32[5,2,32,128]{3,2,1,0:T(8,128)S(1)}, f32[5,2,32,128]{3,2,1,0:T(8,128)S(1)}, u32[]{:S(2)}, u32[]{:S(2)}) %collective-permute-start.4) | collective-permute-done | bytes 163872 | tf_op jit(solution)/shard_map/ppermute | solution.py:218
  10.0 0.5 stencil.1
  10.5 22.7 %all_to_all.18 = f32[32,1280,1]{1,2,0:T(1,128)S(1)} all-to-all(f32[32,1280,1]{1,2,0:T(1,128)S(1)} %bitcast.9), channel_id=1, replica_groups=mesh['phi'=32,'row'=2,'theta'=4] {'phi'}, dimensions={0} | all-to-all | bytes 327680 | tf_op jit(solution)/shard_map/all_to_all | solution.py:229
  33.2 0.2 rotate.1
  33.4 14.3 %all_to_all.19 = f32[32,1280,1]{1,2,0:T(1,128)S(1)} all-to-all(f32[32,1280,1]{1,2,0:T(1,128)S(1)} %bitcast.8), channel_id=1, replica_groups=mesh['phi'=32,'row'=2,'theta'=4] {'phi'}, dimensions={0} | all-to-all | bytes 327680 | tf_op jit(solution)/shard_map/all_to_all | solution.py:229
  47.7 0.7 %unpack.1 = (f32[4,16,128]{2,1,0:T(8,128)}, f32[4,16,128]{2,1,0:T(8,128)}, f32[3,4,16,128]{3,2,1,0:T(8,128)}) custom-call(f32[320,128]{1,0:T(8,128)S(1)} %bitcast.7), custom_call_target="tpu_custom_call" | custom-call | tf_op jit(solution)/shard_map/unpack/pallas_call | solution.py:245
  (4 shorter events, 0.1 us)
Async XLA Ops:
  0.6 1.7 %collective-permute-start = (f32[4,16,128]{2,1,0:T(8,128)}, f32[4,16,128]{2,1,0:T(8,128)S(1)}, u32[]{:S(2)}, u32[]{:S(2)}) collective-permute-start(f32[4,16,128]{2,1,0:T(8,128)} %rho_ref.1), channel_id=1, source_target_pairs={{0,4},{4,0},{1,5},{5,1},{2,6},{6,2},{3,7},{7,3},{8,12},{12,8},{9,1... | collective-permute-start | bytes 98312 | tf_op jit(solution)/shard_map/ppermute | solution.py:193
  0.7 1.6 %collective-permute-start.1 = (f32[4,16,128]{2,1,0:T(8,128)}, f32[4,16,128]{2,1,0:T(8,128)S(1)}, u32[]{:S(2)}, u32[]{:S(2)}) collective-permute-start(f32[4,16,128]{2,1,0:T(8,128)} %en_ref.1), channel_id=1, source_target_pairs={{0,4},{4,0},{1,5},{5,1},{2,6},{6,2},{3,7},{7,3},{8,12},{12,8},{9,1... | collective-permute-start | bytes 98312 | tf_op jit(solution)/shard_map/ppermute | solution.py:194
  1.2 1.5 %collective-permute-start.2 = (f32[3,4,16,128]{3,2,1,0:T(8,128)}, f32[3,4,16,128]{3,2,1,0:T(8,128)S(1)}, u32[]{:S(2)}, u32[]{:S(2)}) collective-permute-start(f32[3,4,16,128]{3,2,1,0:T(8,128)} %vel_ref.1), channel_id=1, source_target_pairs={{0,4},{4,0},{1,5},{5,1},{2,6},{6,2},{3,7},{7,3},{8,12},{12,8},{9,1... | collective-permute-start | bytes 294920 | tf_op jit(solution)/shard_map/ppermute | solution.py:195
  2.8 4.8 %collective-permute-start.3 = (f32[5,2,32,128]{3,2,1,0:T(8,128)S(1)}, f32[5,2,32,128]{3,2,1,0:T(8,128)S(1)}, u32[]{:S(2)}, u32[]{:S(2)}) collective-permute-start(f32[5,2,32,128]{3,2,1,0:T(8,128)S(1)} %maximum_select_fusion), channel_id=1, source_target_pairs={{4,1},{5,2},{6,3},{7,0},{1,4},{2,5},{3,6},{0,7},{12,9},{13,10},{14... | collective-permute-start | bytes 491528 | tf_op jit(solution)/shard_map/ppermute | solution.py:217
  7.6 2.4 %collective-permute-start.4 = (f32[5,2,32,128]{3,2,1,0:T(8,128)S(1)}, f32[5,2,32,128]{3,2,1,0:T(8,128)S(1)}, u32[]{:S(2)}, u32[]{:S(2)}) collective-permute-start(f32[5,2,32,128]{3,2,1,0:T(8,128)S(1)} %collective-permute-done.3.got_ref), channel_id=1, source_target_pairs={{0,4},{4,0},{1,5},{5,1},{2,6},{6,2},{3,7},{7,3},{8,12},{12,8},{9,1... | collective-permute-start | bytes 491528 | tf_op jit(solution)/shard_map/ppermute | solution.py:218

commit v5 on v4

--- a/solution.py
+++ b/solution.py
@@ -70,33 +70,23 @@
         copy.wait()
 
 
-def stencil_kernel(own_ref, sib_ref, got_ref, passed_ref, out_ref):
+def stencil_kernel(own_ref, lo_ref, hi_ref, side_ref, out_ref):
     row = lax.axis_index("row")
     theta = lax.axis_index("theta")
     pos = lax.broadcasted_iota(jnp.int32, (TILE, LANES), 0)
     near = jnp.where(row == 0, pos, TILE - 1 - pos) < TILE // 2
-
-    def halo(f, t, low):
-        parts = []
-        for start, size in ((CR * row, CR), (CR - TILE * row, TILE)):
-            span = pl.ds(pl.multiple_of(start, TILE), size)
-            got, passed = got_ref[f, t, span, :], passed_ref[f, t, span, :]
-            parts.append(jnp.where((row == 0) == low, got, passed))
-        return parts
-
     near = jnp.concatenate([jnp.ones((CR, LANES), jnp.bool_), near], 0)
     below = near & (theta > 0)
     above = near & (theta < lax.axis_size("theta") - 1)
 
     def wide(f, t):
         if t < 2:
-            inside, parts = below, halo(f, t, True)
+            inside, own = below, lo_ref[f, t]
         elif t >= TH + 2:
-            inside, parts = above, halo(f, t - TH - 2, False)
+            inside, own = above, hi_ref[f, t - TH - 2]
         else:
-            side = sib_ref[f, t - 2, pl.ds(pl.multiple_of(TILE * row, TILE), TILE), :]
-            inside, parts = near, [own_ref[f, t - 2], side]
-        return jnp.where(inside, jnp.concatenate(parts, 0), 0.0)
+            inside, own = near, own_ref[f, t - 2]
+        return jnp.where(inside, jnp.concatenate([own, side_ref[f, t]], 0), 0.0)
 
     field = [[wide(f, t) for t in range(TH + 4)] for f in range(FIELDS)]
     first = [[None] * (TH + 4) for _ in range(FIELDS)]
@@ -187,15 +177,6 @@
 def per_device(density, energy, velocity, shifts, viscosity):
     thetas = lax.axis_size("theta")
     row = lax.axis_index("row")
-    swap = [(0, 1), (1, 0)]
-    sibling = jnp.concatenate(
-        [
-            lax.ppermute(density, "row", swap)[None],
-            lax.ppermute(energy, "row", swap)[None],
-            lax.ppermute(velocity, "row", swap),
-        ],
-        0,
-    )
     fields, hops, nu = pl.pallas_call(
         pack_kernel,
         out_shape=(
@@ -208,14 +189,13 @@
         scratch_shapes=[pltpu.SemaphoreType.DMA((5,))],
         name="pack",
     )(density, energy, velocity, shifts, viscosity)
-    outer = jnp.where(
-        row == 0,
-        jnp.concatenate([fields[:, :2], sibling[:, :2]], 2),
-        jnp.concatenate([sibling[:, TH - 2 :], fields[:, TH - 2 :]], 2),
-    )
-    across = [(thetas + i, (i + 1) % thetas) for i in range(thetas)]
-    got = lax.ppermute(outer, ("row", "theta"), across + [(j, i) for i, j in across])
-    passed = lax.ppermute(got, "row", swap)
+    upward = [(i, (i + 1) % thetas) for i in range(thetas)]
+    downward = [(j, i) for i, j in upward]
+    lo = lax.ppermute(fields[:, TH - 2 :], "theta", upward)
+    hi = lax.ppermute(fields[:, :2], "theta", downward)
+    tall = jnp.concatenate([lo, fields, hi], 1)
+    edge = jnp.where(row == 0, tall[:, :, CR - TILE :], tall[:, :, :TILE])
+    side = lax.ppermute(edge, "row", [(0, 1), (1, 0)])
     flat = pltpu.VMEM((PHI * ROWS, LANES), jnp.float32)
     second = pl.pallas_call(
         stencil_kernel,
@@ -223,7 +203,7 @@
         in_specs=[vmem()] * 4,
         out_specs=vmem(),
         name="stencil",
-    )(near(fields), near(sibling), near(got), near(passed))
+    )(near(fields), near(lo), near(hi), near(side))
 
     def exchange(value):
         value = lax.all_to_all(value.reshape(-1), "phi", 0, 0, tiled=True)

time: 48.5 us -> 47.6 us (0.981)
  blocking collectives: 36.9 us -> 35 us
  waiting for transfers between devices: 5.66 us -> 6.94 us
    all_to_all x2, blocking collectives: 36.9 us -> 35 us  [exchange(): value = lax.all_to_all(value.reshape(-1), 'phi', 0, 0, tiled=True)]
    ppermute x5 -> x3, waiting for transfers between devices: 5.66 us -> 6.94 us  [the longest x1 3.15 us: per_device(): hi = lax.ppermute(fields[:, :2], 'theta', downward)]
    ppermute x5 -> x3, starting transfers between devices: 2.64 us -> 2.2 us  [the longest x1 2.04 us: per_device(): lo = lax.ppermute(fields[:, TH - 2:], 'theta', upward)]
  transfers between devices with their start and end apart: 5 -> 3, of which waited for: 3 -> 3; matrix products, arithmetic and copies ran while one was open for 0% -> 0% of each run, Pallas kernels for 2% -> 0%
where the time goes in v5:
time: 47.6 us; the launch traced here: 47.2 us
  blocking collectives  35 us (74%)
  waiting for transfers between devices  6.94 us (15%)
  Pallas kernels  2.34 us (5%)
  starting transfers between devices  2.2 us (5%)
  between operations  0.68 us (1%)
    all_to_all x2, blocking collectives, exchange(): value = lax.all_to_all(value.reshape(-1), 'phi', 0, 0, tiled=True)  35 us
    ppermute x1, waiting for transfers between devices, per_device(): hi = lax.ppermute(fields[:, :2], 'theta', downward)  3.15 us
    ppermute x1, waiting for transfers between devices, per_device(): lo = lax.ppermute(fields[:, TH - 2:], 'theta', upward)  2.41 us
    ppermute x1, starting transfers between devices, per_device(): lo = lax.ppermute(fields[:, TH - 2:], 'theta', upward)  2.04 us
    ppermute x1, waiting for transfers between devices, per_device(): side = lax.ppermute(edge, 'row', [(0, 1), (1, 0)])  1.38 us
    pallas_call x1, Pallas kernels, per_device(): pl.pallas_call(pack_kernel, out_shape=(pltpu.VMEM((FIELDS,) + density.sha...  0.98 us
  transfers between devices with their start and end apart: 3, of which 3 were waited for; matrix products, arithmetic and copies ran while one was open for 0% of the time, Pallas kernels for 0%

profile of v5, /device:TPU:24, one launch (start us, length us, event | category | flops | bytes accessed | tf_op | source)
XLA Modules:
  0.0 47.2 jit_solution(12683146551846450673)
XLA Ops:
  0.6 1.0 %pack.1 = (f32[5,4,16,128]{3,2,1,0:T(8,128)S(1)}, s32[16]{0:T(128)S(4)}, f32[16]{0:T(128)S(4)}) custom-call(f32[4,16,128]{2,1,0:T(8,128)} %rho_ref.1, f32[4,16,128]{2,1,0:T(8,128)} %en_ref.1, f32[3,4,16,128]{3,2,1,0:T(8,128)} %vel_ref.1, s32[16]{0:T(128)} %shift_ref.1, f32[16]{0:T(128)} %visc_ref.1), custom_call_target="tpu_custom_call" | custom-call | tf_op jit(solution)/shard_map/pack/pallas_call | solution.py:180
  1.6 2.0 %collective-permute-start = (f32[5,2,16,128]{3,2,1,0:T(8,128)S(1)}, f32[5,2,16,128]{3,2,1,0:T(8,128)S(1)}, u32[]{:S(2)}, u32[]{:S(2)}) collective-permute-start(f32[5,2,16,128]{3,2,1,0:T(8,128)S(1)} %get-tuple-element.10), channel_id=1, source_target_pairs={{0,1},{1,2},{2,3},{3,0},{4,5},{5,6},{6,7},{7,4},{8,9},{9,10},{10,1... | collective-permute-start | bytes 245768 | tf_op jit(solution)/shard_map/ppermute | solution.py:194
  3.7 0.1 collective-permute-start.1
  3.7 2.4 %collective-permute-done.lo_ref = f32[5,2,16,128]{3,2,1,0:T(8,128)S(1)} collective-permute-done((f32[5,2,16,128]{3,2,1,0:T(8,128)S(1)}, f32[5,2,16,128]{3,2,1,0:T(8,128)S(1)}, u32[]{:S(2)}, u32[]{:S(2)}) %collective-permute-start) | collective-permute-done | bytes 81952 | tf_op jit(solution)/shard_map/ppermute | solution.py:194
  6.2 3.1 %collective-permute-done.1.hi_ref = f32[5,2,16,128]{3,2,1,0:T(8,128)S(1)} collective-permute-done((f32[5,2,16,128]{3,2,1,0:T(8,128)S(1)}, f32[5,2,16,128]{3,2,1,0:T(8,128)S(1)}, u32[]{:S(2)}, u32[]{:S(2)}) %collective-permute-start.1) | collective-permute-done | bytes 81952 | tf_op jit(solution)/shard_map/ppermute | solution.py:195
  9.4 0.1 collective-permute-start.2
  9.5 1.4 %collective-permute-done.2.side_ref = f32[5,8,8,128]{3,2,1,0:T(8,128)S(1)} collective-permute-done((f32[5,8,8,128]{3,2,1,0:T(8,128)S(1)}, f32[5,8,8,128]{3,2,1,0:T(8,128)S(1)}, u32[]{:S(2)}, u32[]{:S(2)}) %collective-permute-start.2) | collective-permute-done | bytes 163872 | tf_op jit(solution)/shard_map/ppermute | solution.py:198
  10.8 0.4 stencil.1
  11.3 20.7 %all_to_all.18 = f32[32,1280,1]{1,2,0:T(1,128)S(1)} all-to-all(f32[32,1280,1]{1,2,0:T(1,128)S(1)} %bitcast.4), channel_id=1, replica_groups=mesh['phi'=32,'row'=2,'theta'=4] {'phi'}, dimensions={0} | all-to-all | bytes 327680 | tf_op jit(solution)/shard_map/all_to_all | solution.py:209
  32.0 0.2 rotate.1
  32.3 14.3 %all_to_all.19 = f32[32,1280,1]{1,2,0:T(1,128)S(1)} all-to-all(f32[32,1280,1]{1,2,0:T(1,128)S(1)} %bitcast.7), channel_id=1, replica_groups=mesh['phi'=32,'row'=2,'theta'=4] {'phi'}, dimensions={0} | all-to-all | bytes 327680 | tf_op jit(solution)/shard_map/all_to_all | solution.py:209
  46.6 0.7 %unpack.1 = (f32[4,16,128]{2,1,0:T(8,128)}, f32[4,16,128]{2,1,0:T(8,128)}, f32[3,4,16,128]{3,2,1,0:T(8,128)}) custom-call(f32[320,128]{1,0:T(8,128)S(1)} %bitcast.6), custom_call_target="tpu_custom_call" | custom-call | tf_op jit(solution)/shard_map/unpack/pallas_call | solution.py:225
  (5 shorter events, 0.1 us)
Async XLA Ops:
  1.6 4.5 %collective-permute-start = (f32[5,2,16,128]{3,2,1,0:T(8,128)S(1)}, f32[5,2,16,128]{3,2,1,0:T(8,128)S(1)}, u32[]{:S(2)}, u32[]{:S(2)}) collective-permute-start(f32[5,2,16,128]{3,2,1,0:T(8,128)S(1)} %get-tuple-element.10), channel_id=1, source_target_pairs={{0,1},{1,2},{2,3},{3,0},{4,5},{5,6},{6,7},{7,4},{8,9},{9,10},{10,1... | collective-permute-start | bytes 245768 | tf_op jit(solution)/shard_map/ppermute | solution.py:194
  3.7 5.7 %collective-permute-start.1 = (f32[5,2,16,128]{3,2,1,0:T(8,128)S(1)}, f32[5,2,16,128]{3,2,1,0:T(8,128)S(1)}, u32[]{:S(2)}, u32[]{:S(2)}) collective-permute-start(f32[5,2,16,128]{3,2,1,0:T(8,128)S(1)} %get-tuple-element.9), channel_id=1, source_target_pairs={{1,0},{2,1},{3,2},{0,3},{5,4},{6,5},{7,6},{4,7},{9,8},{10,9},{11,1... | collective-permute-start | bytes 245768 | tf_op jit(solution)/shard_map/ppermute | solution.py:195
  9.4 1.5 %collective-permute-start.2 = (f32[5,8,8,128]{3,2,1,0:T(8,128)S(1)}, f32[5,8,8,128]{3,2,1,0:T(8,128)S(1)}, u32[]{:S(2)}, u32[]{:S(2)}) collective-permute-start(f32[5,8,8,128]{3,2,1,0:T(8,128)S(1)} %slice_select_fusion), channel_id=1, source_target_pairs={{0,4},{4,0},{1,5},{5,1},{2,6},{6,2},{3,7},{7,3},{8,12},{12,8},{9,1... | collective-permute-start | bytes 491528 | tf_op jit(solution)/shard_map/ppermute | solution.py:198

commit v6 on v5

--- a/solution.py
+++ b/solution.py
@@ -74,7 +74,9 @@
     row = lax.axis_index("row")
     theta = lax.axis_index("theta")
     pos = lax.broadcasted_iota(jnp.int32, (TILE, LANES), 0)
-    near = jnp.where(row == 0, pos, TILE - 1 - pos) < TILE // 2
+    first_pos = jnp.where(row == 0, 0, TILE - 2)
+    at_first, at_second = pos == first_pos, pos == first_pos + 1
+    near = at_first | at_second
     near = jnp.concatenate([jnp.ones((CR, LANES), jnp.bool_), near], 0)
     below = near & (theta > 0)
     above = near & (theta < lax.axis_size("theta") - 1)
@@ -86,7 +88,9 @@
             inside, own = above, hi_ref[f, t - TH - 2]
         else:
             inside, own = near, own_ref[f, t - 2]
-        return jnp.where(inside, jnp.concatenate([own, side_ref[f, t]], 0), 0.0)
+        one = jnp.broadcast_to(side_ref[f, t, :1], (TILE, LANES))
+        two = jnp.broadcast_to(side_ref[f, t, 1:], (TILE, LANES))
+        return jnp.where(inside, jnp.concatenate([own, jnp.where(at_first, one, two)], 0), 0.0)
 
     field = [[wide(f, t) for t in range(TH + 4)] for f in range(FIELDS)]
     first = [[None] * (TH + 4) for _ in range(FIELDS)]
@@ -194,7 +198,7 @@
     lo = lax.ppermute(fields[:, TH - 2 :], "theta", upward)
     hi = lax.ppermute(fields[:, :2], "theta", downward)
     tall = jnp.concatenate([lo, fields, hi], 1)
-    edge = jnp.where(row == 0, tall[:, :, CR - TILE :], tall[:, :, :TILE])
+    edge = jnp.where(row == 0, tall[:, :, CR - 2 :], tall[:, :, :2])
     side = lax.ppermute(edge, "row", [(0, 1), (1, 0)])
     flat = pltpu.VMEM((PHI * ROWS, LANES), jnp.float32)
     second = pl.pallas_call(

time: 47.6 us -> 47.4 us (level)
  no operation moved by 1% of the time
where the time goes in v6:
time: 47.4 us; the launch traced here: 47.1 us
  blocking collectives  35 us (74%)
  waiting for transfers between devices  6.77 us (14%)
  Pallas kernels  2.36 us (5%)
  starting transfers between devices  2.2 us (5%)
  between operations  0.68 us (1%)
    all_to_all x2, blocking collectives, exchange(): value = lax.all_to_all(value.reshape(-1), 'phi', 0, 0, tiled=True)  35 us
    ppermute x1, waiting for transfers between devices, per_device(): hi = lax.ppermute(fields[:, :2], 'theta', downward)  3.15 us
    ppermute x1, waiting for transfers between devices, per_device(): lo = lax.ppermute(fields[:, TH - 2:], 'theta', upward)  2.41 us
    ppermute x1, starting transfers between devices, per_device(): lo = lax.ppermute(fields[:, TH - 2:], 'theta', upward)  2.04 us
    ppermute x1, waiting for transfers between devices, per_device(): side = lax.ppermute(edge, 'row', [(0, 1), (1, 0)])  1.21 us
    pallas_call x1, Pallas kernels, per_device(): pl.pallas_call(pack_kernel, out_shape=(pltpu.VMEM((FIELDS,) + density.sha...  0.98 us
  transfers between devices with their start and end apart: 3, of which 3 were waited for; matrix products, arithmetic and copies ran while one was open for 0% of the time, Pallas kernels for 0%

profile of v6, /device:TPU:24, one launch (start us, length us, event | category | flops | bytes accessed | tf_op | source)
XLA Modules:
  0.0 47.1 jit_solution(3416184909895899898)
XLA Ops:
  0.6 1.0 %pack.1 = (f32[5,4,16,128]{3,2,1,0:T(8,128)S(1)}, s32[16]{0:T(128)S(4)}, f32[16]{0:T(128)S(4)}) custom-call(f32[4,16,128]{2,1,0:T(8,128)} %rho_ref.1, f32[4,16,128]{2,1,0:T(8,128)} %en_ref.1, f32[3,4,16,128]{3,2,1,0:T(8,128)} %vel_ref.1, s32[16]{0:T(128)} %shift_ref.1, f32[16]{0:T(128)} %visc_ref.1), custom_call_target="tpu_custom_call" | custom-call | tf_op jit(solution)/shard_map/pack/pallas_call | solution.py:184
  1.6 2.0 %collective-permute-start = (f32[5,2,16,128]{3,2,1,0:T(8,128)S(1)}, f32[5,2,16,128]{3,2,1,0:T(8,128)S(1)}, u32[]{:S(2)}, u32[]{:S(2)}) collective-permute-start(f32[5,2,16,128]{3,2,1,0:T(8,128)S(1)} %get-tuple-element.10), channel_id=1, source_target_pairs={{0,1},{1,2},{2,3},{3,0},{4,5},{5,6},{6,7},{7,4},{8,9},{9,10},{10,1... | collective-permute-start | bytes 245768 | tf_op jit(solution)/shard_map/ppermute | solution.py:198
  3.7 0.1 collective-permute-start.1
  3.7 2.4 %collective-permute-done.lo_ref = f32[5,2,16,128]{3,2,1,0:T(8,128)S(1)} collective-permute-done((f32[5,2,16,128]{3,2,1,0:T(8,128)S(1)}, f32[5,2,16,128]{3,2,1,0:T(8,128)S(1)}, u32[]{:S(2)}, u32[]{:S(2)}) %collective-permute-start) | collective-permute-done | bytes 81952 | tf_op jit(solution)/shard_map/ppermute | solution.py:198
  6.2 3.1 %collective-permute-done.1.hi_ref = f32[5,2,16,128]{3,2,1,0:T(8,128)S(1)} collective-permute-done((f32[5,2,16,128]{3,2,1,0:T(8,128)S(1)}, f32[5,2,16,128]{3,2,1,0:T(8,128)S(1)}, u32[]{:S(2)}, u32[]{:S(2)}) %collective-permute-start.1) | collective-permute-done | bytes 81952 | tf_op jit(solution)/shard_map/ppermute | solution.py:199
  9.4 0.1 collective-permute-start.2
  9.5 1.2 %collective-permute-done.2.side_ref = f32[5,8,2,128]{3,2,1,0:T(2,128)S(1)} collective-permute-done((f32[5,8,2,128]{3,2,1,0:T(2,128)S(1)}, f32[5,8,2,128]{3,2,1,0:T(2,128)S(1)}, u32[]{:S(2)}, u32[]{:S(2)}) %collective-permute-start.2) | collective-permute-done | bytes 40992 | tf_op jit(solution)/shard_map/ppermute | solution.py:202
  10.7 0.5 stencil.1
  11.1 20.8 %all_to_all.18 = f32[32,1280,1]{1,2,0:T(1,128)S(1)} all-to-all(f32[32,1280,1]{1,2,0:T(1,128)S(1)} %bitcast.4), channel_id=1, replica_groups=mesh['phi'=32,'row'=2,'theta'=4] {'phi'}, dimensions={0} | all-to-all | bytes 327680 | tf_op jit(solution)/shard_map/all_to_all | solution.py:213
  31.9 0.2 rotate.1
  32.1 14.3 %all_to_all.19 = f32[32,1280,1]{1,2,0:T(1,128)S(1)} all-to-all(f32[32,1280,1]{1,2,0:T(1,128)S(1)} %bitcast.7), channel_id=1, replica_groups=mesh['phi'=32,'row'=2,'theta'=4] {'phi'}, dimensions={0} | all-to-all | bytes 327680 | tf_op jit(solution)/shard_map/all_to_all | solution.py:213
  46.4 0.7 %unpack.1 = (f32[4,16,128]{2,1,0:T(8,128)}, f32[4,16,128]{2,1,0:T(8,128)}, f32[3,4,16,128]{3,2,1,0:T(8,128)}) custom-call(f32[320,128]{1,0:T(8,128)S(1)} %bitcast.6), custom_call_target="tpu_custom_call" | custom-call | tf_op jit(solution)/shard_map/unpack/pallas_call | solution.py:229
  (5 shorter events, 0.1 us)
Async XLA Ops:
  1.6 4.5 %collective-permute-start = (f32[5,2,16,128]{3,2,1,0:T(8,128)S(1)}, f32[5,2,16,128]{3,2,1,0:T(8,128)S(1)}, u32[]{:S(2)}, u32[]{:S(2)}) collective-permute-start(f32[5,2,16,128]{3,2,1,0:T(8,128)S(1)} %get-tuple-element.10), channel_id=1, source_target_pairs={{0,1},{1,2},{2,3},{3,0},{4,5},{5,6},{6,7},{7,4},{8,9},{9,10},{10,1... | collective-permute-start | bytes 245768 | tf_op jit(solution)/shard_map/ppermute | solution.py:198
  3.7 5.7 %collective-permute-start.1 = (f32[5,2,16,128]{3,2,1,0:T(8,128)S(1)}, f32[5,2,16,128]{3,2,1,0:T(8,128)S(1)}, u32[]{:S(2)}, u32[]{:S(2)}) collective-permute-start(f32[5,2,16,128]{3,2,1,0:T(8,128)S(1)} %get-tuple-element.9), channel_id=1, source_target_pairs={{1,0},{2,1},{3,2},{0,3},{5,4},{6,5},{7,6},{4,7},{9,8},{10,9},{11,1... | collective-permute-start | bytes 245768 | tf_op jit(solution)/shard_map/ppermute | solution.py:199
  9.4 1.3 %collective-permute-start.2 = (f32[5,8,2,128]{3,2,1,0:T(2,128)S(1)}, f32[5,8,2,128]{3,2,1,0:T(2,128)S(1)}, u32[]{:S(2)}, u32[]{:S(2)}) collective-permute-start(f32[5,8,2,128]{3,2,1,0:T(2,128)S(1)} %slice_select_fusion), channel_id=1, source_target_pairs={{0,4},{4,0},{1,5},{5,1},{2,6},{6,2},{3,7},{7,3},{8,12},{12,8},{9,1... | collective-permute-start | bytes 122888 | tf_op jit(solution)/shard_map/ppermute | solution.py:202

commit v7 on v5

--- a/solution.py
+++ b/solution.py
@@ -18,6 +18,7 @@
 PHI = 32
 PAIRS = TH * CR // PHI
 ROWS = FIELDS * PAIRS
+BODY = FIELDS * 2 * CR
 
 
 def face(q_lo, q_hi, u_lo, u_hi):
@@ -70,23 +71,50 @@
         copy.wait()
 
 
-def stencil_kernel(own_ref, lo_ref, hi_ref, side_ref, out_ref):
+def side_of(refs, f, t):
+    return refs[0].at[t] if f == 0 else refs[1].at[t] if f == 1 else refs[2].at[f - 2, t]
+
+
+def build_kernel(own_ref, sib_rho, sib_en, sib_vel, up_ref, down_ref):
+    border = (CR - 1) * lax.axis_index("row")
+    sib = (sib_rho, sib_en, sib_vel)
+    for out_ref, low, corner in ((up_ref, TH - 2, TH - 1), (down_ref, 0, 0)):
+        out_ref[BODY:] = jnp.zeros((TILE, LANES), jnp.float32)
+        for f in range(FIELDS):
+            for t in range(2):
+                out_ref[(2 * f + t) * CR : (2 * f + t + 1) * CR] = own_ref[f, low + t]
+            out_ref[BODY + f : BODY + f + 1] = side_of(sib, f, corner)[pl.ds(border, 1), :]
+
+
+def stencil_kernel(own_ref, sib_rho, sib_en, sib_vel, lo_ref, hi_ref, out_ref):
     row = lax.axis_index("row")
     theta = lax.axis_index("theta")
+    sib = (sib_rho, sib_en, sib_vel)
     pos = lax.broadcasted_iota(jnp.int32, (TILE, LANES), 0)
-    near = jnp.where(row == 0, pos, TILE - 1 - pos) < TILE // 2
-    near = jnp.concatenate([jnp.ones((CR, LANES), jnp.bool_), near], 0)
+    first_pos = (TILE - 2) * row
+    at_first, at_second = pos == first_pos, pos == first_pos + 1
+    at_border = pos == (TILE - 1) * row
+    near = jnp.concatenate([jnp.ones((CR, LANES), jnp.bool_), at_border], 0)
     below = near & (theta > 0)
     above = near & (theta < lax.axis_size("theta") - 1)
+    nothing = jnp.zeros((TILE, LANES), jnp.float32)
+
+    def spread(line):
+        return jnp.broadcast_to(line, (TILE, LANES))
 
     def wide(f, t):
-        if t < 2:
-            inside, own = below, lo_ref[f, t]
-        elif t >= TH + 2:
-            inside, own = above, hi_ref[f, t - TH - 2]
-        else:
-            inside, own = near, own_ref[f, t - 2]
-        return jnp.where(inside, jnp.concatenate([own, side_ref[f, t]], 0), 0.0)
+        if 2 <= t < TH + 2:
+            side = side_of(sib, f, t - 2)
+            one = spread(side[pl.ds((CR - 2) * row, 1), :])
+            two = spread(side[pl.ds((CR - 2) * row + 1, 1), :])
+            tile = jnp.where(at_first, one, jnp.where(at_second, two, nothing))
+            return jnp.concatenate([own_ref[f, t - 2], tile], 0)
+        ref, inside = (lo_ref, below) if t < 2 else (hi_ref, above)
+        start = (2 * f + t % 2) * CR
+        tile = nothing
+        if t in (1, TH + 2):
+            tile = spread(ref[BODY + f : BODY + f + 1])
+        return jnp.where(inside, jnp.concatenate([ref[start : start + CR], tile], 0), 0.0)
 
     field = [[wide(f, t) for t in range(TH + 4)] for f in range(FIELDS)]
     first = [[None] * (TH + 4) for _ in range(FIELDS)]
@@ -177,6 +205,9 @@
 def per_device(density, energy, velocity, shifts, viscosity):
     thetas = lax.axis_size("theta")
     row = lax.axis_index("row")
+    swap = [(0, 1), (1, 0)]
+    sibling = [near(lax.ppermute(value, "row", swap)) for value in (velocity, density, energy)]
+    sibling = sibling[1:] + sibling[:1]
     fields, hops, nu = pl.pallas_call(
         pack_kernel,
         out_shape=(
@@ -191,19 +222,24 @@
     )(density, energy, velocity, shifts, viscosity)
     upward = [(i, (i + 1) % thetas) for i in range(thetas)]
     downward = [(j, i) for i, j in upward]
-    lo = lax.ppermute(fields[:, TH - 2 :], "theta", upward)
-    hi = lax.ppermute(fields[:, :2], "theta", downward)
-    tall = jnp.concatenate([lo, fields, hi], 1)
-    edge = jnp.where(row == 0, tall[:, :, CR - TILE :], tall[:, :, :TILE])
-    side = lax.ppermute(edge, "row", [(0, 1), (1, 0)])
+    message = pltpu.VMEM((BODY + TILE, LANES), jnp.float32)
+    last, first = pl.pallas_call(
+        build_kernel,
+        out_shape=(message, message),
+        in_specs=[vmem()] * 4,
+        out_specs=(vmem(), vmem()),
+        name="build",
+    )(near(fields), *sibling)
+    lo = lax.ppermute(last, "theta", upward)
+    hi = lax.ppermute(first, "theta", downward)
     flat = pltpu.VMEM((PHI * ROWS, LANES), jnp.float32)
     second = pl.pallas_call(
         stencil_kernel,
         out_shape=flat,
-        in_specs=[vmem()] * 4,
+        in_specs=[vmem()] * 6,
         out_specs=vmem(),
         name="stencil",
-    )(near(fields), near(lo), near(hi), near(side))
+    )(near(fields), *sibling, near(lo), near(hi))
 
     def exchange(value):
         value = lax.all_to_all(value.reshape(-1), "phi", 0, 0, tiled=True)

time: 47.6 us -> 46.4 us (0.975)
  waiting for transfers between devices: 6.94 us -> 5.96 us
  blocking collectives: 35 us -> 34.4 us
  starting transfers between devices: 2.2 us -> 2.79 us
    ppermute x3 -> x5, waiting for transfers between devices: 6.94 us -> 5.96 us  [the longest x1 3.05 us: per_device(): hi = lax.ppermute(first, 'theta', downward)]
    all_to_all x2, blocking collectives: 35 us -> 34.4 us  [exchange(): value = lax.all_to_all(value.reshape(-1), 'phi', 0, 0, tiled=True)]
    ppermute x3 -> x5, starting transfers between devices: 2.2 us -> 2.79 us  [the longest x1 2.04 us: per_device(): lo = lax.ppermute(last, 'theta', upward)]
  transfers between devices with their start and end apart: 3 -> 5, of which waited for: 3 -> 3; matrix products, arithmetic and copies ran while one was open for 0% -> 0% of each run, Pallas kernels for 0% -> 2%
where the time goes in v7:
time: 46.4 us; the launch traced here: 46.2 us
  blocking collectives  34.4 us (74%)
  waiting for transfers between devices  5.96 us (13%)
  starting transfers between devices  2.79 us (6%)
  Pallas kernels  2.36 us (5%)
  between operations  0.67 us (1%)
    all_to_all x2, blocking collectives, exchange(): value = lax.all_to_all(value.reshape(-1), 'phi', 0, 0, tiled=True)  34.4 us
    ppermute x1, waiting for transfers between devices, per_device(): hi = lax.ppermute(first, 'theta', downward)  3.05 us
    ppermute x1, waiting for transfers between devices, per_device(): lo = lax.ppermute(last, 'theta', upward)  2.57 us
    ppermute x1, starting transfers between devices, per_device(): lo = lax.ppermute(last, 'theta', upward)  2.04 us
    pallas_call x1, Pallas kernels, per_device(): pl.pallas_call(pack_kernel, out_shape=(pltpu.VMEM((FIELDS,) + density.sha...  0.98 us
  transfers between devices with their start and end apart: 5, of which 3 were waited for; matrix products, arithmetic and copies ran while one was open for 0% of the time, Pallas kernels for 2%

profile of v7, /device:TPU:24, one launch (start us, length us, event | category | flops | bytes accessed | tf_op | source)
XLA Modules:
  0.0 46.2 jit_solution(3713052280413774297)
XLA Ops:
  0.6 0.1 collective-permute-start.2
  0.7 0.5 %collective-permute-start = (f32[4,16,128]{2,1,0:T(8,128)}, f32[4,16,128]{2,1,0:T(8,128)S(1)}, u32[]{:S(2)}, u32[]{:S(2)}) collective-permute-start(f32[4,16,128]{2,1,0:T(8,128)} %rho_ref.1), channel_id=1, source_target_pairs={{0,4},{4,0},{1,5},{5,1},{2,6},{6,2},{3,7},{7,3},{8,12},{12,8},{9,1... | collective-permute-start | bytes 98312 | tf_op jit(solution)/shard_map/ppermute | solution.py:209
  1.2 0.1 collective-permute-start.1
  1.3 1.0 %pack.1 = (f32[5,4,16,128]{3,2,1,0:T(8,128)S(1)}, s32[16]{0:T(128)S(4)}, f32[16]{0:T(128)S(4)}) custom-call(f32[4,16,128]{2,1,0:T(8,128)} %rho_ref.1, f32[4,16,128]{2,1,0:T(8,128)} %en_ref.1, f32[3,4,16,128]{3,2,1,0:T(8,128)} %vel_ref.1, s32[16]{0:T(128)} %shift_ref.1, f32[16]{0:T(128)} %visc_ref.1), custom_call_target="tpu_custom_call" | custom-call | tf_op jit(solution)/shard_map/pack/pallas_call | solution.py:211
  2.3 0.0 collective-permute-done.sib_rho
  2.3 0.3 collective-permute-done.1.sib_en
  2.6 0.0 collective-permute-done.2.sib_vel
  2.7 2.0 %collective-permute-start.3 = (f32[168,128]{1,0:T(8,128)S(1)}, f32[168,128]{1,0:T(8,128)S(1)}, u32[]{:S(2)}, u32[]{:S(2)}) collective-permute-start(f32[168,128]{1,0:T(8,128)S(1)} %get-tuple-element.11), channel_id=1, source_target_pairs={{0,1},{1,2},{2,3},{3,0},{4,5},{5,6},{6,7},{7,4},{8,9},{9,10},{10,1... | collective-permute-start | bytes 258056 | tf_op jit(solution)/shard_map/ppermute | solution.py:233
  4.7 0.1 collective-permute-start.4
  4.8 2.6 %collective-permute-done.3.lo_ref = f32[168,128]{1,0:T(8,128)S(1)} collective-permute-done((f32[168,128]{1,0:T(8,128)S(1)}, f32[168,128]{1,0:T(8,128)S(1)}, u32[]{:S(2)}, u32[]{:S(2)}) %collective-permute-start.3) | collective-permute-done | bytes 86048 | tf_op jit(solution)/shard_map/ppermute | solution.py:233
  7.3 3.1 %collective-permute-done.4.hi_ref = f32[168,128]{1,0:T(8,128)S(1)} collective-permute-done((f32[168,128]{1,0:T(8,128)S(1)}, f32[168,128]{1,0:T(8,128)S(1)}, u32[]{:S(2)}, u32[]{:S(2)}) %collective-permute-start.4) | collective-permute-done | bytes 86048 | tf_op jit(solution)/shard_map/ppermute | solution.py:234
  10.4 0.5 stencil.1
  10.9 20.3 %all_to_all.18 = f32[32,1280,1]{1,2,0:T(1,128)S(1)} all-to-all(f32[32,1280,1]{1,2,0:T(1,128)S(1)} %bitcast.7), channel_id=1, replica_groups=mesh['phi'=32,'row'=2,'theta'=4] {'phi'}, dimensions={0} | all-to-all | bytes 327680 | tf_op jit(solution)/shard_map/all_to_all | solution.py:245
  31.1 0.2 rotate.1
  31.4 14.1 %all_to_all.19 = f32[32,1280,1]{1,2,0:T(1,128)S(1)} all-to-all(f32[32,1280,1]{1,2,0:T(1,128)S(1)} %bitcast.6), channel_id=1, replica_groups=mesh['phi'=32,'row'=2,'theta'=4] {'phi'}, dimensions={0} | all-to-all | bytes 327680 | tf_op jit(solution)/shard_map/all_to_all | solution.py:245
  45.5 0.7 %unpack.1 = (f32[4,16,128]{2,1,0:T(8,128)}, f32[4,16,128]{2,1,0:T(8,128)}, f32[3,4,16,128]{3,2,1,0:T(8,128)}) custom-call(f32[320,128]{1,0:T(8,128)S(1)} %bitcast.5), custom_call_target="tpu_custom_call" | custom-call | tf_op jit(solution)/shard_map/unpack/pallas_call | solution.py:261
  (1 shorter events, 0.0 us)
Async XLA Ops:
  0.6 2.0 %collective-permute-start.2 = (f32[3,4,16,128]{3,2,1,0:T(8,128)}, f32[3,4,16,128]{3,2,1,0:T(8,128)S(1)}, u32[]{:S(2)}, u32[]{:S(2)}) collective-permute-start(f32[3,4,16,128]{3,2,1,0:T(8,128)} %vel_ref.1), channel_id=1, source_target_pairs={{0,4},{4,0},{1,5},{5,1},{2,6},{6,2},{3,7},{7,3},{8,12},{12,8},{9,1... | collective-permute-start | bytes 294920 | tf_op jit(solution)/shard_map/ppermute | solution.py:209
  0.7 1.6 %collective-permute-start = (f32[4,16,128]{2,1,0:T(8,128)}, f32[4,16,128]{2,1,0:T(8,128)S(1)}, u32[]{:S(2)}, u32[]{:S(2)}) collective-permute-start(f32[4,16,128]{2,1,0:T(8,128)} %rho_ref.1), channel_id=1, source_target_pairs={{0,4},{4,0},{1,5},{5,1},{2,6},{6,2},{3,7},{7,3},{8,12},{12,8},{9,1... | collective-permute-start | bytes 98312 | tf_op jit(solution)/shard_map/ppermute | solution.py:209
  1.2 1.4 %collective-permute-start.1 = (f32[4,16,128]{2,1,0:T(8,128)}, f32[4,16,128]{2,1,0:T(8,128)S(1)}, u32[]{:S(2)}, u32[]{:S(2)}) collective-permute-start(f32[4,16,128]{2,1,0:T(8,128)} %en_ref.1), channel_id=1, source_target_pairs={{0,4},{4,0},{1,5},{5,1},{2,6},{6,2},{3,7},{7,3},{8,12},{12,8},{9,1... | collective-permute-start | bytes 98312 | tf_op jit(solution)/shard_map/ppermute | solution.py:209
  2.7 4.7 %collective-permute-start.3 = (f32[168,128]{1,0:T(8,128)S(1)}, f32[168,128]{1,0:T(8,128)S(1)}, u32[]{:S(2)}, u32[]{:S(2)}) collective-permute-start(f32[168,128]{1,0:T(8,128)S(1)} %get-tuple-element.11), channel_id=1, source_target_pairs={{0,1},{1,2},{2,3},{3,0},{4,5},{5,6},{6,7},{7,4},{8,9},{9,10},{10,1... | collective-permute-start | bytes 258056 | tf_op jit(solution)/shard_map/ppermute | solution.py:233
  4.7 5.7 %collective-permute-start.4 = (f32[168,128]{1,0:T(8,128)S(1)}, f32[168,128]{1,0:T(8,128)S(1)}, u32[]{:S(2)}, u32[]{:S(2)}) collective-permute-start(f32[168,128]{1,0:T(8,128)S(1)} %get-tuple-element.12), channel_id=1, source_target_pairs={{1,0},{2,1},{3,2},{0,3},{5,4},{6,5},{7,6},{4,7},{9,8},{10,9},{11,1... | collective-permute-start | bytes 258056 | tf_op jit(solution)/shard_map/ppermute | solution.py:234

commit v8 on v7

--- a/solution.py
+++ b/solution.py
@@ -86,47 +86,75 @@
             out_ref[BODY + f : BODY + f + 1] = side_of(sib, f, corner)[pl.ds(border, 1), :]
 
 
-def stencil_kernel(own_ref, sib_rho, sib_en, sib_vel, lo_ref, hi_ref, out_ref):
-    row = lax.axis_index("row")
-    theta = lax.axis_index("theta")
-    sib = (sib_rho, sib_en, sib_vel)
-    pos = lax.broadcasted_iota(jnp.int32, (TILE, LANES), 0)
-    first_pos = (TILE - 2) * row
-    at_first, at_second = pos == first_pos, pos == first_pos + 1
-    at_border = pos == (TILE - 1) * row
-    near = jnp.concatenate([jnp.ones((CR, LANES), jnp.bool_), at_border], 0)
-    below = near & (theta > 0)
-    above = near & (theta < lax.axis_size("theta") - 1)
-    nothing = jnp.zeros((TILE, LANES), jnp.float32)
-
-    def spread(line):
-        return jnp.broadcast_to(line, (TILE, LANES))
-
-    def wide(f, t):
+class Block:
+    def __init__(self, own_ref, sib, lo_ref=None, hi_ref=None):
+        row = lax.axis_index("row")
+        theta = lax.axis_index("theta")
+        self.row, self.own_ref, self.sib, self.halo = row, own_ref, sib, (lo_ref, hi_ref)
+        pos = lax.broadcasted_iota(jnp.int32, (TILE, LANES), 0)
+        first_pos = (TILE - 2) * row
+        self.at_first, self.at_second = pos == first_pos, pos == first_pos + 1
+        at_border = pos == (TILE - 1) * row
+        self.near = jnp.concatenate([jnp.ones((CR, LANES), jnp.bool_), at_border], 0)
+        self.below = self.near & (theta > 0)
+        self.above = self.near & (theta < lax.axis_size("theta") - 1)
+        self.nothing = jnp.zeros((TILE, LANES), jnp.float32)
+
+    def inside(self, t):
+        return self.below if t < 2 else self.above if t >= TH + 2 else self.near
+
+    def wide(self, f, t):
         if 2 <= t < TH + 2:
-            side = side_of(sib, f, t - 2)
-            one = spread(side[pl.ds((CR - 2) * row, 1), :])
-            two = spread(side[pl.ds((CR - 2) * row + 1, 1), :])
-            tile = jnp.where(at_first, one, jnp.where(at_second, two, nothing))
-            return jnp.concatenate([own_ref[f, t - 2], tile], 0)
-        ref, inside = (lo_ref, below) if t < 2 else (hi_ref, above)
+            side = side_of(self.sib, f, t - 2)
+            one = spread(side[pl.ds((CR - 2) * self.row, 1), :])
+            two = spread(side[pl.ds((CR - 2) * self.row + 1, 1), :])
+            tile = jnp.where(self.at_first, one, jnp.where(self.at_second, two, self.nothing))
+            return jnp.concatenate([self.own_ref[f, t - 2], tile], 0)
+        ref = self.halo[t >= 2]
         start = (2 * f + t % 2) * CR
-        tile = nothing
+        tile = self.nothing
         if t in (1, TH + 2):
             tile = spread(ref[BODY + f : BODY + f + 1])
-        return jnp.where(inside, jnp.concatenate([ref[start : start + CR], tile], 0), 0.0)
-
-    field = [[wide(f, t) for t in range(TH + 4)] for f in range(FIELDS)]
+        whole = jnp.concatenate([ref[start : start + CR], tile], 0)
+        return jnp.where(self.inside(t), whole, 0.0)
+
+    def inverse(self, field, t):
+        return 1.0 / jnp.where(self.inside(t), field[0][t], 1.0)
+
+    def first(self, field, inverse, t):
+        steps = rates(field, inverse, t)
+        return [jnp.where(self.inside(t), field[f][t] + TIME_STEP * steps[f], 0.0) for f in range(FIELDS)]
+
+
+def spread(line):
+    return jnp.broadcast_to(line, (TILE, LANES))
+
+
+def inner_kernel(own_ref, sib_rho, sib_en, sib_vel, first_ref, inv_ref):
+    block = Block(own_ref, (sib_rho, sib_en, sib_vel))
+    field = [[block.wide(f, t) if 2 <= t < TH + 2 else None for t in range(TH + 4)] for f in range(FIELDS)]
+    for t in range(2, TH + 2):
+        inverse = block.inverse(field, t)
+        inv_ref[t - 2] = inverse
+        if 2 < t < TH + 1:
+            for f, value in enumerate(block.first(field, inverse, t)):
+                first_ref[f, t - 3] = value
+
+
+def stencil_kernel(own_ref, sib_rho, sib_en, sib_vel, lo_ref, hi_ref, first_ref, inv_ref, out_ref):
+    block = Block(own_ref, (sib_rho, sib_en, sib_vel), lo_ref, hi_ref)
+    field = [[block.wide(f, t) for t in range(TH + 4)] for f in range(FIELDS)]
     first = [[None] * (TH + 4) for _ in range(FIELDS)]
-    inverse = [None] * (TH + 4)
     for t in range(1, TH + 3):
-        inside = below if t == 1 else above if t == TH + 2 else near
-        inverse[t] = 1.0 / jnp.where(inside, field[0][t], 1.0)
-        steps = rates(field, inverse[t], t)
+        if 2 < t < TH + 1:
+            values = [first_ref[f, t - 3] for f in range(FIELDS)]
+        else:
+            inverse = inv_ref[t - 2] if 2 <= t < TH + 2 else block.inverse(field, t)
+            values = block.first(field, inverse, t)
         for f in range(FIELDS):
-            first[f][t] = jnp.where(inside, field[f][t] + TIME_STEP * steps[f], 0.0)
+            first[f][t] = values[f]
     for t in range(2, TH + 2):
-        steps = rates(first, inverse[t], t)
+        steps = rates(first, inv_ref[t - 2], t)
         for f in range(FIELDS):
             second = 0.5 * (field[f][t] + first[f][t] + TIME_STEP * steps[f])
             for p in range(PAIRS):
@@ -232,14 +260,25 @@
     )(near(fields), *sibling)
     lo = lax.ppermute(last, "theta", upward)
     hi = lax.ppermute(first, "theta", downward)
+    tall = CR + TILE
+    first_one, inverse = pl.pallas_call(
+        inner_kernel,
+        out_shape=(
+            pltpu.VMEM((FIELDS, TH - 2, tall, LANES), jnp.float32),
+            pltpu.VMEM((TH, tall, LANES), jnp.float32),
+        ),
+        in_specs=[vmem()] * 4,
+        out_specs=(vmem(), vmem()),
+        name="inner",
+    )(near(fields), *sibling)
     flat = pltpu.VMEM((PHI * ROWS, LANES), jnp.float32)
     second = pl.pallas_call(
         stencil_kernel,
         out_shape=flat,
-        in_specs=[vmem()] * 6,
+        in_specs=[vmem()] * 8,
         out_specs=vmem(),
         name="stencil",
-    )(near(fields), *sibling, near(lo), near(hi))
+    )(near(fields), *sibling, near(lo), near(hi), near(first_one), near(inverse))
 
     def exchange(value):
         value = lax.all_to_all(value.reshape(-1), "phi", 0, 0, tiled=True)

time: 46.4 us -> 46.3 us (level)
  no operation moved by 1% of the time
where the time goes in v8:
time: 46.3 us; the launch traced here: 46.1 us
  blocking collectives  34.4 us (74%)
  waiting for transfers between devices  5.84 us (13%)
  starting transfers between devices  2.79 us (6%)
  Pallas kernels  2.38 us (5%)
  between operations  0.67 us (1%)
    all_to_all x2, blocking collectives, exchange(): value = lax.all_to_all(value.reshape(-1), 'phi', 0, 0, tiled=True)  34.4 us
    ppermute x1, waiting for transfers between devices, per_device(): hi = lax.ppermute(first, 'theta', downward)  3.05 us
    ppermute x1, waiting for transfers between devices, per_device(): lo = lax.ppermute(last, 'theta', upward)  2.46 us
    ppermute x1, starting transfers between devices, per_device(): lo = lax.ppermute(last, 'theta', upward)  2.04 us
    pallas_call x1, Pallas kernels, per_device(): pl.pallas_call(pack_kernel, out_shape=(pltpu.VMEM((FIELDS,) + density.sha...  0.98 us
  transfers between devices with their start and end apart: 5, of which 3 were waited for; matrix products, arithmetic and copies ran while one was open for 0% of the time, Pallas kernels for 2%

profile of v8, /device:TPU:24, one launch (start us, length us, event | category | flops | bytes accessed | tf_op | source)
XLA Modules:
  0.0 46.1 jit_solution(18369137904443479640)
XLA Ops:
  0.6 0.1 collective-permute-start.2
  0.7 0.5 %collective-permute-start = (f32[4,16,128]{2,1,0:T(8,128)}, f32[4,16,128]{2,1,0:T(8,128)S(1)}, u32[]{:S(2)}, u32[]{:S(2)}) collective-permute-start(f32[4,16,128]{2,1,0:T(8,128)} %rho_ref.1), channel_id=1, source_target_pairs={{0,4},{4,0},{1,5},{5,1},{2,6},{6,2},{3,7},{7,3},{8,12},{12,8},{9,1... | collective-permute-start | bytes 98312 | tf_op jit(solution)/shard_map/ppermute | solution.py:237
  1.2 0.1 collective-permute-start.1
  1.3 1.0 %pack.1 = (f32[5,4,16,128]{3,2,1,0:T(8,128)S(1)}, s32[16]{0:T(128)S(4)}, f32[16]{0:T(128)S(4)}) custom-call(f32[4,16,128]{2,1,0:T(8,128)} %rho_ref.1, f32[4,16,128]{2,1,0:T(8,128)} %en_ref.1, f32[3,4,16,128]{3,2,1,0:T(8,128)} %vel_ref.1, s32[16]{0:T(128)} %shift_ref.1, f32[16]{0:T(128)} %visc_ref.1), custom_call_target="tpu_custom_call" | custom-call | tf_op jit(solution)/shard_map/pack/pallas_call | solution.py:239
  2.3 0.0 collective-permute-done.sib_rho
  2.3 0.3 collective-permute-done.1.sib_en
  2.6 0.0 collective-permute-done.2.sib_vel
  2.7 2.0 %collective-permute-start.3 = (f32[168,128]{1,0:T(8,128)S(1)}, f32[168,128]{1,0:T(8,128)S(1)}, u32[]{:S(2)}, u32[]{:S(2)}) collective-permute-start(f32[168,128]{1,0:T(8,128)S(1)} %get-tuple-element.13), channel_id=1, source_target_pairs={{0,1},{1,2},{2,3},{3,0},{4,5},{5,6},{6,7},{7,4},{8,9},{9,10},{10,1... | collective-permute-start | bytes 258056 | tf_op jit(solution)/shard_map/ppermute | solution.py:261
  4.7 0.1 collective-permute-start.4
  4.8 0.1 inner.1
  4.9 2.5 %collective-permute-done.3.lo_ref = f32[168,128]{1,0:T(8,128)S(1)} collective-permute-done((f32[168,128]{1,0:T(8,128)S(1)}, f32[168,128]{1,0:T(8,128)S(1)}, u32[]{:S(2)}, u32[]{:S(2)}) %collective-permute-start.3) | collective-permute-done | bytes 86048 | tf_op jit(solution)/shard_map/ppermute | solution.py:261
  7.3 3.1 %collective-permute-done.4.hi_ref = f32[168,128]{1,0:T(8,128)S(1)} collective-permute-done((f32[168,128]{1,0:T(8,128)S(1)}, f32[168,128]{1,0:T(8,128)S(1)}, u32[]{:S(2)}, u32[]{:S(2)}) %collective-permute-start.4) | collective-permute-done | bytes 86048 | tf_op jit(solution)/shard_map/ppermute | solution.py:262
  10.4 0.4 stencil.1
  10.8 20.2 %all_to_all.18 = f32[32,1280,1]{1,2,0:T(1,128)S(1)} all-to-all(f32[32,1280,1]{1,2,0:T(1,128)S(1)} %bitcast.4), channel_id=1, replica_groups=mesh['phi'=32,'row'=2,'theta'=4] {'phi'}, dimensions={0} | all-to-all | bytes 327680 | tf_op jit(solution)/shard_map/all_to_all | solution.py:284
  31.0 0.2 rotate.1
  31.3 14.1 %all_to_all.19 = f32[32,1280,1]{1,2,0:T(1,128)S(1)} all-to-all(f32[32,1280,1]{1,2,0:T(1,128)S(1)} %bitcast.7), channel_id=1, replica_groups=mesh['phi'=32,'row'=2,'theta'=4] {'phi'}, dimensions={0} | all-to-all | bytes 327680 | tf_op jit(solution)/shard_map/all_to_all | solution.py:284
  45.4 0.7 %unpack.1 = (f32[4,16,128]{2,1,0:T(8,128)}, f32[4,16,128]{2,1,0:T(8,128)}, f32[3,4,16,128]{3,2,1,0:T(8,128)}) custom-call(f32[320,128]{1,0:T(8,128)S(1)} %bitcast.6), custom_call_target="tpu_custom_call" | custom-call | tf_op jit(solution)/shard_map/unpack/pallas_call | solution.py:300
  (1 shorter events, 0.0 us)
Async XLA Ops:
  0.6 2.0 %collective-permute-start.2 = (f32[3,4,16,128]{3,2,1,0:T(8,128)}, f32[3,4,16,128]{3,2,1,0:T(8,128)S(1)}, u32[]{:S(2)}, u32[]{:S(2)}) collective-permute-start(f32[3,4,16,128]{3,2,1,0:T(8,128)} %vel_ref.1), channel_id=1, source_target_pairs={{0,4},{4,0},{1,5},{5,1},{2,6},{6,2},{3,7},{7,3},{8,12},{12,8},{9,1... | collective-permute-start | bytes 294920 | tf_op jit(solution)/shard_map/ppermute | solution.py:237
  0.7 1.6 %collective-permute-start = (f32[4,16,128]{2,1,0:T(8,128)}, f32[4,16,128]{2,1,0:T(8,128)S(1)}, u32[]{:S(2)}, u32[]{:S(2)}) collective-permute-start(f32[4,16,128]{2,1,0:T(8,128)} %rho_ref.1), channel_id=1, source_target_pairs={{0,4},{4,0},{1,5},{5,1},{2,6},{6,2},{3,7},{7,3},{8,12},{12,8},{9,1... | collective-permute-start | bytes 98312 | tf_op jit(solution)/shard_map/ppermute | solution.py:237
  1.2 1.4 %collective-permute-start.1 = (f32[4,16,128]{2,1,0:T(8,128)}, f32[4,16,128]{2,1,0:T(8,128)S(1)}, u32[]{:S(2)}, u32[]{:S(2)}) collective-permute-start(f32[4,16,128]{2,1,0:T(8,128)} %en_ref.1), channel_id=1, source_target_pairs={{0,4},{4,0},{1,5},{5,1},{2,6},{6,2},{3,7},{7,3},{8,12},{12,8},{9,1... | collective-permute-start | bytes 98312 | tf_op jit(solution)/shard_map/ppermute | solution.py:237
  2.7 4.7 %collective-permute-start.3 = (f32[168,128]{1,0:T(8,128)S(1)}, f32[168,128]{1,0:T(8,128)S(1)}, u32[]{:S(2)}, u32[]{:S(2)}) collective-permute-start(f32[168,128]{1,0:T(8,128)S(1)} %get-tuple-element.13), channel_id=1, source_target_pairs={{0,1},{1,2},{2,3},{3,0},{4,5},{5,6},{6,7},{7,4},{8,9},{9,10},{10,1... | collective-permute-start | bytes 258056 | tf_op jit(solution)/shard_map/ppermute | solution.py:261
  4.7 5.7 %collective-permute-start.4 = (f32[168,128]{1,0:T(8,128)S(1)}, f32[168,128]{1,0:T(8,128)S(1)}, u32[]{:S(2)}, u32[]{:S(2)}) collective-permute-start(f32[168,128]{1,0:T(8,128)S(1)} %get-tuple-element.14), channel_id=1, source_target_pairs={{1,0},{2,1},{3,2},{0,3},{5,4},{6,5},{7,6},{4,7},{9,8},{10,9},{11,1... | collective-permute-start | bytes 258056 | tf_op jit(solution)/shard_map/ppermute | solution.py:262

commit v9 on v8

--- a/solution.py
+++ b/solution.py
@@ -162,7 +162,7 @@
                 out_ref[pl.ds(start, TILE, stride=ROWS), :] = second[p * TILE : (p + 1) * TILE]
 
 
-def rotate_kernel(shift_ref, visc_ref, in_ref, out_ref, twice_ref):
+def rotate_kernel(shift_ref, visc_ref, in_ref, out_ref):
     mine = lax.axis_index("phi") % TILE
     lane = lax.broadcasted_iota(jnp.int32, (PHI, LANES), 1)
     for p in range(PAIRS):
@@ -175,12 +175,8 @@
 
         def shifted(f):
             turned = pltpu.roll(in_ref[pl.ds(f * PAIRS + p, PHI, stride=ROWS), :], rest, 1)
-            slot = f * PAIRS + p
-            twice_ref[slot, :PHI] = turned
-            twice_ref[slot, PHI:] = turned
-            near = twice_ref[slot, pl.ds(PHI - hops, PHI), :]
-            far = twice_ref[slot, pl.ds(PHI - 1 - hops, PHI), :]
-            return jnp.where(wrapped, far, near)
+            near = pltpu.roll(turned, hops, 0)
+            return jnp.where(wrapped, pltpu.roll(near, 1, 0), near)
 
         def put(f, value):
             out_ref[pl.ds(f * PAIRS + p, PHI, stride=ROWS), :] = value
@@ -289,7 +285,6 @@
         out_shape=flat,
         in_specs=[smem(), smem(), vmem()],
         out_specs=vmem(),
-        scratch_shapes=[pltpu.VMEM((ROWS, 2 * PHI, LANES), jnp.float32)],
         name="rotate",
     )(
         pltpu.with_memory_space_constraint(hops, pltpu.SMEM),

time: 46.3 us -> 46.2 us (level)
  no operation moved by 1% of the time
where the time goes in v9:
time: 46.2 us; the launch traced here: 46 us
  blocking collectives  34.4 us (74%)
  waiting for transfers between devices  5.84 us (13%)
  starting transfers between devices  2.79 us (6%)
  Pallas kernels  2.34 us (5%)
  between operations  0.67 us (1%)
    all_to_all x2, blocking collectives, exchange(): value = lax.all_to_all(value.reshape(-1), 'phi', 0, 0, tiled=True)  34.4 us
    ppermute x1, waiting for transfers between devices, per_device(): hi = lax.ppermute(first, 'theta', downward)  3.05 us
    ppermute x1, waiting for transfers between devices, per_device(): lo = lax.ppermute(last, 'theta', upward)  2.46 us
    ppermute x1, starting transfers between devices, per_device(): lo = lax.ppermute(last, 'theta', upward)  2.04 us
    pallas_call x1, Pallas kernels, per_device(): pl.pallas_call(pack_kernel, out_shape=(pltpu.VMEM((FIELDS,) + density.sha...  0.98 us
  transfers between devices with their start and end apart: 5, of which 3 were waited for; matrix products, arithmetic and copies ran while one was open for 0% of the time, Pallas kernels for 2%

profile of v9, /device:TPU:24, one launch (start us, length us, event | category | flops | bytes accessed | tf_op | source)
XLA Modules:
  0.0 46.0 jit_solution(9447224918804962719)
XLA Ops:
  0.6 0.1 collective-permute-start.2
  0.7 0.5 %collective-permute-start = (f32[4,16,128]{2,1,0:T(8,128)}, f32[4,16,128]{2,1,0:T(8,128)S(1)}, u32[]{:S(2)}, u32[]{:S(2)}) collective-permute-start(f32[4,16,128]{2,1,0:T(8,128)} %rho_ref.1), channel_id=1, source_target_pairs={{0,4},{4,0},{1,5},{5,1},{2,6},{6,2},{3,7},{7,3},{8,12},{12,8},{9,1... | collective-permute-start | bytes 98312 | tf_op jit(solution)/shard_map/ppermute | solution.py:233
  1.2 0.1 collective-permute-start.1
  1.3 1.0 %pack.1 = (f32[5,4,16,128]{3,2,1,0:T(8,128)S(1)}, s32[16]{0:T(128)S(4)}, f32[16]{0:T(128)S(4)}) custom-call(f32[4,16,128]{2,1,0:T(8,128)} %rho_ref.1, f32[4,16,128]{2,1,0:T(8,128)} %en_ref.1, f32[3,4,16,128]{3,2,1,0:T(8,128)} %vel_ref.1, s32[16]{0:T(128)} %shift_ref.1, f32[16]{0:T(128)} %visc_ref.1), custom_call_target="tpu_custom_call" | custom-call | tf_op jit(solution)/shard_map/pack/pallas_call | solution.py:235
  2.3 0.0 collective-permute-done.sib_rho
  2.3 0.3 collective-permute-done.1.sib_en
  2.6 0.0 collective-permute-done.2.sib_vel
  2.7 2.0 %collective-permute-start.3 = (f32[168,128]{1,0:T(8,128)S(1)}, f32[168,128]{1,0:T(8,128)S(1)}, u32[]{:S(2)}, u32[]{:S(2)}) collective-permute-start(f32[168,128]{1,0:T(8,128)S(1)} %get-tuple-element.13), channel_id=1, source_target_pairs={{0,1},{1,2},{2,3},{3,0},{4,5},{5,6},{6,7},{7,4},{8,9},{9,10},{10,1... | collective-permute-start | bytes 258056 | tf_op jit(solution)/shard_map/ppermute | solution.py:257
  4.7 0.1 collective-permute-start.4
  4.8 0.1 inner.1
  4.9 2.5 %collective-permute-done.3.lo_ref = f32[168,128]{1,0:T(8,128)S(1)} collective-permute-done((f32[168,128]{1,0:T(8,128)S(1)}, f32[168,128]{1,0:T(8,128)S(1)}, u32[]{:S(2)}, u32[]{:S(2)}) %collective-permute-start.3) | collective-permute-done | bytes 86048 | tf_op jit(solution)/shard_map/ppermute | solution.py:257
  7.3 3.1 %collective-permute-done.4.hi_ref = f32[168,128]{1,0:T(8,128)S(1)} collective-permute-done((f32[168,128]{1,0:T(8,128)S(1)}, f32[168,128]{1,0:T(8,128)S(1)}, u32[]{:S(2)}, u32[]{:S(2)}) %collective-permute-start.4) | collective-permute-done | bytes 86048 | tf_op jit(solution)/shard_map/ppermute | solution.py:258
  10.4 0.4 stencil.1
  10.8 20.2 %all_to_all.18 = f32[32,1280,1]{1,2,0:T(1,128)S(1)} all-to-all(f32[32,1280,1]{1,2,0:T(1,128)S(1)} %bitcast.4), channel_id=1, replica_groups=mesh['phi'=32,'row'=2,'theta'=4] {'phi'}, dimensions={0} | all-to-all | bytes 327680 | tf_op jit(solution)/shard_map/all_to_all | solution.py:280
  31.0 0.2 rotate.1
  31.2 14.1 %all_to_all.19 = f32[32,1280,1]{1,2,0:T(1,128)S(1)} all-to-all(f32[32,1280,1]{1,2,0:T(1,128)S(1)} %bitcast.7), channel_id=1, replica_groups=mesh['phi'=32,'row'=2,'theta'=4] {'phi'}, dimensions={0} | all-to-all | bytes 327680 | tf_op jit(solution)/shard_map/all_to_all | solution.py:280
  45.4 0.7 %unpack.1 = (f32[4,16,128]{2,1,0:T(8,128)}, f32[4,16,128]{2,1,0:T(8,128)}, f32[3,4,16,128]{3,2,1,0:T(8,128)}) custom-call(f32[320,128]{1,0:T(8,128)S(1)} %bitcast.6), custom_call_target="tpu_custom_call" | custom-call | tf_op jit(solution)/shard_map/unpack/pallas_call | solution.py:295
  (1 shorter events, 0.0 us)
Async XLA Ops:
  0.6 2.0 %collective-permute-start.2 = (f32[3,4,16,128]{3,2,1,0:T(8,128)}, f32[3,4,16,128]{3,2,1,0:T(8,128)S(1)}, u32[]{:S(2)}, u32[]{:S(2)}) collective-permute-start(f32[3,4,16,128]{3,2,1,0:T(8,128)} %vel_ref.1), channel_id=1, source_target_pairs={{0,4},{4,0},{1,5},{5,1},{2,6},{6,2},{3,7},{7,3},{8,12},{12,8},{9,1... | collective-permute-start | bytes 294920 | tf_op jit(solution)/shard_map/ppermute | solution.py:233
  0.7 1.6 %collective-permute-start = (f32[4,16,128]{2,1,0:T(8,128)}, f32[4,16,128]{2,1,0:T(8,128)S(1)}, u32[]{:S(2)}, u32[]{:S(2)}) collective-permute-start(f32[4,16,128]{2,1,0:T(8,128)} %rho_ref.1), channel_id=1, source_target_pairs={{0,4},{4,0},{1,5},{5,1},{2,6},{6,2},{3,7},{7,3},{8,12},{12,8},{9,1... | collective-permute-start | bytes 98312 | tf_op jit(solution)/shard_map/ppermute | solution.py:233
  1.2 1.4 %collective-permute-start.1 = (f32[4,16,128]{2,1,0:T(8,128)}, f32[4,16,128]{2,1,0:T(8,128)S(1)}, u32[]{:S(2)}, u32[]{:S(2)}) collective-permute-start(f32[4,16,128]{2,1,0:T(8,128)} %en_ref.1), channel_id=1, source_target_pairs={{0,4},{4,0},{1,5},{5,1},{2,6},{6,2},{3,7},{7,3},{8,12},{12,8},{9,1... | collective-permute-start | bytes 98312 | tf_op jit(solution)/shard_map/ppermute | solution.py:233
  2.7 4.7 %collective-permute-start.3 = (f32[168,128]{1,0:T(8,128)S(1)}, f32[168,128]{1,0:T(8,128)S(1)}, u32[]{:S(2)}, u32[]{:S(2)}) collective-permute-start(f32[168,128]{1,0:T(8,128)S(1)} %get-tuple-element.13), channel_id=1, source_target_pairs={{0,1},{1,2},{2,3},{3,0},{4,5},{5,6},{6,7},{7,4},{8,9},{9,10},{10,1... | collective-permute-start | bytes 258056 | tf_op jit(solution)/shard_map/ppermute | solution.py:257
  4.7 5.7 %collective-permute-start.4 = (f32[168,128]{1,0:T(8,128)S(1)}, f32[168,128]{1,0:T(8,128)S(1)}, u32[]{:S(2)}, u32[]{:S(2)}) collective-permute-start(f32[168,128]{1,0:T(8,128)S(1)} %get-tuple-element.14), channel_id=1, source_target_pairs={{1,0},{2,1},{3,2},{0,3},{5,4},{6,5},{7,6},{4,7},{9,8},{10,9},{11,1... | collective-permute-start | bytes 258056 | tf_op jit(solution)/shard_map/ppermute | solution.py:258

commit v10 on v9

--- a/solution.py
+++ b/solution.py
@@ -33,28 +33,44 @@
     return pltpu.roll(value, 1, 0)
 
 
-def rates(field, inv_rho, t):
+def rates(field, inv_rho, t, skip=0):
     rho, en, vr, vt, vp = (field[f] for f in range(FIELDS))
     vr_hi = up(vr[t])
-    out = []
+
+    def at(q, step):
+        return 0.0 if step == skip else q[t + step]
 
     def divergence(q, q_hi):
         flux = face(q[t], q_hi, vr[t], vr_hi)
-        radial = flux - down(flux)
-        polar = face(q[t], q[t + 1], vt[t], vt[t + 1]) - face(q[t - 1], q[t], vt[t - 1], vt[t])
-        return radial + polar
+        total = flux - down(flux)
+        if skip != 1:
+            total = total + face(q[t], q[t + 1], vt[t], vt[t + 1])
+        if skip != -1:
+            total = total - face(q[t - 1], q[t], vt[t - 1], vt[t])
+        return total
 
     en_hi = up(en[t])
     d_rho = -divergence(rho, up(rho[t]))
     d_en = -divergence(en, en_hi)
     d_vp = -divergence(vp, up(vp[t])) - 0.5 * ROTATION * vr[t]
     grad_r = 0.5 * GAMMA_LESS * (en_hi - down(en[t]))
-    grad_t = 0.5 * GAMMA_LESS * (en[t + 1] - en[t - 1])
-    lap_r = vr[t + 1] + vr[t - 1] + vr_hi + down(vr[t]) - 4.0 * vr[t]
-    lap_t = vt[t + 1] + vt[t - 1] + up(vt[t]) + down(vt[t]) - 4.0 * vt[t]
+    grad_t = 0.5 * GAMMA_LESS * (at(en, 1) - at(en, -1))
+    lap_r = at(vr, 1) + at(vr, -1) + vr_hi + down(vr[t]) - 4.0 * vr[t]
+    lap_t = at(vt, 1) + at(vt, -1) + up(vt[t]) + down(vt[t]) - 4.0 * vt[t]
     d_vr = -grad_r * inv_rho + 0.5 * DAMPING * lap_r + 2.0 * ROTATION * vp[t]
     d_vt = -grad_t * inv_rho + 0.5 * DAMPING * lap_t
     return d_rho, d_en, d_vr, d_vt, d_vp
+
+
+def neighbour_rates(field, inv_rho, t, step):
+    _, en, vr, vt, _ = (field[f] for f in range(FIELDS))
+    lo, hi = min(t, t + step), max(t, t + step)
+
+    def flux(q):
+        return -step * face(q[lo], q[hi], vt[lo], vt[hi])
+
+    d_vt = 0.5 * DAMPING * vt[t + step] - step * 0.5 * GAMMA_LESS * en[t + step] * inv_rho
+    return flux(field[0]), flux(en), 0.5 * DAMPING * vr[t + step], d_vt, flux(field[4])
 
 
 def pack_kernel(rho_ref, en_ref, vel_ref, shift_ref, visc_ref, out_ref, hop_ref, nu_ref, sems):
@@ -87,7 +103,7 @@
 
 
 class Block:
-    def __init__(self, own_ref, sib, lo_ref=None, hi_ref=None):
+    def __init__(self, own_ref=None, sib=None, lo_ref=None, hi_ref=None):
         row = lax.axis_index("row")
         theta = lax.axis_index("theta")
         self.row, self.own_ref, self.sib, self.halo = row, own_ref, sib, (lo_ref, hi_ref)
@@ -121,8 +137,8 @@
     def inverse(self, field, t):
         return 1.0 / jnp.where(self.inside(t), field[0][t], 1.0)
 
-    def first(self, field, inverse, t):
-        steps = rates(field, inverse, t)
+    def first(self, field, inverse, t, skip=0):
+        steps = rates(field, inverse, t, skip)
         return [jnp.where(self.inside(t), field[f][t] + TIME_STEP * steps[f], 0.0) for f in range(FIELDS)]
 
 
@@ -130,27 +146,35 @@
     return jnp.broadcast_to(line, (TILE, LANES))
 
 
-def inner_kernel(own_ref, sib_rho, sib_en, sib_vel, first_ref, inv_ref):
+def inner_kernel(own_ref, sib_rho, sib_en, sib_vel, wide_ref, first_ref, inv_ref):
     block = Block(own_ref, (sib_rho, sib_en, sib_vel))
     field = [[block.wide(f, t) if 2 <= t < TH + 2 else None for t in range(TH + 4)] for f in range(FIELDS)]
     for t in range(2, TH + 2):
         inverse = block.inverse(field, t)
         inv_ref[t - 2] = inverse
-        if 2 < t < TH + 1:
-            for f, value in enumerate(block.first(field, inverse, t)):
-                first_ref[f, t - 3] = value
-
-
-def stencil_kernel(own_ref, sib_rho, sib_en, sib_vel, lo_ref, hi_ref, first_ref, inv_ref, out_ref):
-    block = Block(own_ref, (sib_rho, sib_en, sib_vel), lo_ref, hi_ref)
-    field = [[block.wide(f, t) for t in range(TH + 4)] for f in range(FIELDS)]
+        for f in range(FIELDS):
+            wide_ref[f, t - 2] = field[f][t]
+        skip = -1 if t == 2 else 1 if t == TH + 1 else 0
+        for f, value in enumerate(block.first(field, inverse, t, skip)):
+            first_ref[f, t - 2] = value
+
+
+def stencil_kernel(lo_ref, hi_ref, wide_ref, first_ref, inv_ref, out_ref):
+    block = Block(lo_ref=lo_ref, hi_ref=hi_ref)
+    field = [
+        [wide_ref[f, t - 2] if 2 <= t < TH + 2 else block.wide(f, t) for t in range(TH + 4)]
+        for f in range(FIELDS)
+    ]
     first = [[None] * (TH + 4) for _ in range(FIELDS)]
     for t in range(1, TH + 3):
-        if 2 < t < TH + 1:
-            values = [first_ref[f, t - 3] for f in range(FIELDS)]
+        if 2 <= t < TH + 2:
+            values = [first_ref[f, t - 2] for f in range(FIELDS)]
+            step = -1 if t == 2 else 1 if t == TH + 1 else 0
+            if step:
+                more = neighbour_rates(field, inv_ref[t - 2], t, step)
+                values = [jnp.where(block.near, v + TIME_STEP * m, 0.0) for v, m in zip(values, more)]
         else:
-            inverse = inv_ref[t - 2] if 2 <= t < TH + 2 else block.inverse(field, t)
-            values = block.first(field, inverse, t)
+            values = block.first(field, block.inverse(field, t), t)
         for f in range(FIELDS):
             first[f][t] = values[f]
     for t in range(2, TH + 2):
@@ -257,24 +281,25 @@
     lo = lax.ppermute(last, "theta", upward)
     hi = lax.ppermute(first, "theta", downward)
     tall = CR + TILE
-    first_one, inverse = pl.pallas_call(
+    wide, first_one, inverse = pl.pallas_call(
         inner_kernel,
         out_shape=(
-            pltpu.VMEM((FIELDS, TH - 2, tall, LANES), jnp.float32),
+            pltpu.VMEM((FIELDS, TH, tall, LANES), jnp.float32),
+            pltpu.VMEM((FIELDS, TH, tall, LANES), jnp.float32),
             pltpu.VMEM((TH, tall, LANES), jnp.float32),
         ),
         in_specs=[vmem()] * 4,
-        out_specs=(vmem(), vmem()),
+        out_specs=(vmem(), vmem(), vmem()),
         name="inner",
     )(near(fields), *sibling)
     flat = pltpu.VMEM((PHI * ROWS, LANES), jnp.float32)
     second = pl.pallas_call(
         stencil_kernel,
         out_shape=flat,
-        in_specs=[vmem()] * 8,
+        in_specs=[vmem()] * 5,
         out_specs=vmem(),
         name="stencil",
-    )(near(fields), *sibling, near(lo), near(hi), near(first_one), near(inverse))
+    )(near(lo), near(hi), near(wide), near(first_one), near(inverse))
 
     def exchange(value):
         value = lax.all_to_all(value.reshape(-1), "phi", 0, 0, tiled=True)

time: 46.2 us -> 46.1 us (level)
  transfers between devices with their start and end apart: 5 -> 5, of which waited for: 3 -> 3; matrix products, arithmetic and copies ran while one was open for 0% -> 0% of each run, Pallas kernels for 2% -> 3%
where the time goes in v10:
time: 46.1 us; the launch traced here: 46 us
  blocking collectives  34.4 us (75%)
  waiting for transfers between devices  5.78 us (13%)
  starting transfers between devices  2.79 us (6%)
  Pallas kernels  2.32 us (5%)
  between operations  0.67 us (1%)
    all_to_all x2, blocking collectives, exchange(): value = lax.all_to_all(value.reshape(-1), 'phi', 0, 0, tiled=True)  34.4 us
    ppermute x1, waiting for transfers between devices, per_device(): hi = lax.ppermute(first, 'theta', downward)  3.05 us
    ppermute x1, waiting for transfers between devices, per_device(): lo = lax.ppermute(last, 'theta', upward)  2.39 us
    ppermute x1, starting transfers between devices, per_device(): lo = lax.ppermute(last, 'theta', upward)  2.04 us
    pallas_call x1, Pallas kernels, per_device(): pl.pallas_call(pack_kernel, out_shape=(pltpu.VMEM((FIELDS,) + density.sha...  0.98 us
  transfers between devices with their start and end apart: 5, of which 3 were waited for; matrix products, arithmetic and copies ran while one was open for 0% of the time, Pallas kernels for 3%

profile of v10, /device:TPU:24, one launch (start us, length us, event | category | flops | bytes accessed | tf_op | source)
XLA Modules:
  0.0 46.0 jit_solution(14818902841884692762)
XLA Ops:
  0.6 0.1 collective-permute-start.2
  0.7 0.5 %collective-permute-start = (f32[4,16,128]{2,1,0:T(8,128)}, f32[4,16,128]{2,1,0:T(8,128)S(1)}, u32[]{:S(2)}, u32[]{:S(2)}) collective-permute-start(f32[4,16,128]{2,1,0:T(8,128)} %rho_ref.1), channel_id=1, source_target_pairs={{0,4},{4,0},{1,5},{5,1},{2,6},{6,2},{3,7},{7,3},{8,12},{12,8},{9,1... | collective-permute-start | bytes 98312 | tf_op jit(solution)/shard_map/ppermute | solution.py:257
  1.2 0.1 collective-permute-start.1
  1.3 1.0 %pack.1 = (f32[5,4,16,128]{3,2,1,0:T(8,128)S(1)}, s32[16]{0:T(128)S(4)}, f32[16]{0:T(128)S(4)}) custom-call(f32[4,16,128]{2,1,0:T(8,128)} %rho_ref.1, f32[4,16,128]{2,1,0:T(8,128)} %en_ref.1, f32[3,4,16,128]{3,2,1,0:T(8,128)} %vel_ref.1, s32[16]{0:T(128)} %shift_ref.1, f32[16]{0:T(128)} %visc_ref.1), custom_call_target="tpu_custom_call" | custom-call | tf_op jit(solution)/shard_map/pack/pallas_call | solution.py:259
  2.3 0.0 collective-permute-done.sib_rho
  2.3 0.3 collective-permute-done.1.sib_en
  2.6 0.0 collective-permute-done.2.sib_vel
  2.7 2.0 %collective-permute-start.3 = (f32[168,128]{1,0:T(8,128)S(1)}, f32[168,128]{1,0:T(8,128)S(1)}, u32[]{:S(2)}, u32[]{:S(2)}) collective-permute-start(f32[168,128]{1,0:T(8,128)S(1)} %get-tuple-element.14), channel_id=1, source_target_pairs={{0,1},{1,2},{2,3},{3,0},{4,5},{5,6},{6,7},{7,4},{8,9},{9,10},{10,1... | collective-permute-start | bytes 258056 | tf_op jit(solution)/shard_map/ppermute | solution.py:281
  4.7 0.1 collective-permute-start.4
  4.8 0.2 inner.1
  5.0 2.4 %collective-permute-done.3.lo_ref = f32[168,128]{1,0:T(8,128)S(1)} collective-permute-done((f32[168,128]{1,0:T(8,128)S(1)}, f32[168,128]{1,0:T(8,128)S(1)}, u32[]{:S(2)}, u32[]{:S(2)}) %collective-permute-start.3) | collective-permute-done | bytes 86048 | tf_op jit(solution)/shard_map/ppermute | solution.py:281
  7.3 3.1 %collective-permute-done.4.hi_ref = f32[168,128]{1,0:T(8,128)S(1)} collective-permute-done((f32[168,128]{1,0:T(8,128)S(1)}, f32[168,128]{1,0:T(8,128)S(1)}, u32[]{:S(2)}, u32[]{:S(2)}) %collective-permute-start.4) | collective-permute-done | bytes 86048 | tf_op jit(solution)/shard_map/ppermute | solution.py:282
  10.4 0.3 stencil.1
  10.7 20.3 %all_to_all.18 = f32[32,1280,1]{1,2,0:T(1,128)S(1)} all-to-all(f32[32,1280,1]{1,2,0:T(1,128)S(1)} %bitcast.7), channel_id=1, replica_groups=mesh['phi'=32,'row'=2,'theta'=4] {'phi'}, dimensions={0} | all-to-all | bytes 327680 | tf_op jit(solution)/shard_map/all_to_all | solution.py:305
  30.9 0.2 rotate.1
  31.1 14.1 %all_to_all.19 = f32[32,1280,1]{1,2,0:T(1,128)S(1)} all-to-all(f32[32,1280,1]{1,2,0:T(1,128)S(1)} %bitcast.6), channel_id=1, replica_groups=mesh['phi'=32,'row'=2,'theta'=4] {'phi'}, dimensions={0} | all-to-all | bytes 327680 | tf_op jit(solution)/shard_map/all_to_all | solution.py:305
  45.3 0.7 %unpack.1 = (f32[4,16,128]{2,1,0:T(8,128)}, f32[4,16,128]{2,1,0:T(8,128)}, f32[3,4,16,128]{3,2,1,0:T(8,128)}) custom-call(f32[320,128]{1,0:T(8,128)S(1)} %bitcast.5), custom_call_target="tpu_custom_call" | custom-call | tf_op jit(solution)/shard_map/unpack/pallas_call | solution.py:320
  (1 shorter events, 0.0 us)
Async XLA Ops:
  0.6 2.0 %collective-permute-start.2 = (f32[3,4,16,128]{3,2,1,0:T(8,128)}, f32[3,4,16,128]{3,2,1,0:T(8,128)S(1)}, u32[]{:S(2)}, u32[]{:S(2)}) collective-permute-start(f32[3,4,16,128]{3,2,1,0:T(8,128)} %vel_ref.1), channel_id=1, source_target_pairs={{0,4},{4,0},{1,5},{5,1},{2,6},{6,2},{3,7},{7,3},{8,12},{12,8},{9,1... | collective-permute-start | bytes 294920 | tf_op jit(solution)/shard_map/ppermute | solution.py:257
  0.7 1.6 %collective-permute-start = (f32[4,16,128]{2,1,0:T(8,128)}, f32[4,16,128]{2,1,0:T(8,128)S(1)}, u32[]{:S(2)}, u32[]{:S(2)}) collective-permute-start(f32[4,16,128]{2,1,0:T(8,128)} %rho_ref.1), channel_id=1, source_target_pairs={{0,4},{4,0},{1,5},{5,1},{2,6},{6,2},{3,7},{7,3},{8,12},{12,8},{9,1... | collective-permute-start | bytes 98312 | tf_op jit(solution)/shard_map/ppermute | solution.py:257
  1.2 1.4 %collective-permute-start.1 = (f32[4,16,128]{2,1,0:T(8,128)}, f32[4,16,128]{2,1,0:T(8,128)S(1)}, u32[]{:S(2)}, u32[]{:S(2)}) collective-permute-start(f32[4,16,128]{2,1,0:T(8,128)} %en_ref.1), channel_id=1, source_target_pairs={{0,4},{4,0},{1,5},{5,1},{2,6},{6,2},{3,7},{7,3},{8,12},{12,8},{9,1... | collective-permute-start | bytes 98312 | tf_op jit(solution)/shard_map/ppermute | solution.py:257
  2.7 4.7 %collective-permute-start.3 = (f32[168,128]{1,0:T(8,128)S(1)}, f32[168,128]{1,0:T(8,128)S(1)}, u32[]{:S(2)}, u32[]{:S(2)}) collective-permute-start(f32[168,128]{1,0:T(8,128)S(1)} %get-tuple-element.14), channel_id=1, source_target_pairs={{0,1},{1,2},{2,3},{3,0},{4,5},{5,6},{6,7},{7,4},{8,9},{9,10},{10,1... | collective-permute-start | bytes 258056 | tf_op jit(solution)/shard_map/ppermute | solution.py:281
  4.7 5.7 %collective-permute-start.4 = (f32[168,128]{1,0:T(8,128)S(1)}, f32[168,128]{1,0:T(8,128)S(1)}, u32[]{:S(2)}, u32[]{:S(2)}) collective-permute-start(f32[168,128]{1,0:T(8,128)S(1)} %get-tuple-element.15), channel_id=1, source_target_pairs={{1,0},{2,1},{3,2},{0,3},{5,4},{6,5},{7,6},{4,7},{9,8},{10,9},{11,1... | collective-permute-start | bytes 258056 | tf_op jit(solution)/shard_map/ppermute | solution.py:282
